TPU v7x, 32 devices: a whole 2x2x4 slice. The times are simulated.
32 devices in a mesh: qrow: 4 (over x, core), kcol: 8 (over z, y).
Axes of the slice: x: 2, y: 2, z: 4, core: 2. Of those that a mesh axis runs over, the one named last changes fastest.
Arguments:
- queries: bfloat16 [4096, 512], P(('qrow', 'kcol')), may hold values from -4.5 to 4.5
- keys: bfloat16 [4096, 128], P(('qrow', 'kcol')), may hold values from -4.5 to 4.5
- values: bfloat16 [4096, 128], P(('qrow', 'kcol')), may hold values from -6 to 6
- upstream: bfloat16 [4096, 512], P(('qrow', 'kcol')), may hold values from -6 to 6
- block_order: int32 [32], replicated, may hold values from 0 to 31, each once
Outputs:
- attended: float32 [4096, 512], P(('qrow', 'kcol'))
- query_grad: float32 [4096, 512], P(('qrow', 'kcol'))
- key_grad: float32 [4096, 128], P(('qrow', 'kcol'))
- value_grad: float32 [4096, 128], P(('qrow', 'kcol'))
Inputs may be any that keep to these rules, and one draw needn't show every extreme that they name: `block_order`: each number appears once.
All inputs are finite; a program needn't handle non-finite values.
Results may differ from a plain program's by a relative error of at most 0.0071.
Values may be sent and summed in bfloat16 or wider, within the bound.
No kernel may reach another device: no remote copies, remote signals or barrier semaphores. Data moves between devices by JAX's collectives and lax.ppermute only.
A program may use at most 64 MiB of HBM per device.

v0:
```python
import math

import jax
import jax.numpy as jnp
from jax import lax
from jax.sharding import PartitionSpec as P


def merged(value, axis, join):
    pieces = jax.tree.map(lambda part: lax.all_gather(part, axis), value)
    head = jax.tree.map(lambda part: part[0], pieces)
    tail = jax.tree.map(lambda part: part[1:], pieces)
    running, _ = lax.scan(lambda running, share: (join(running, share), None), head, tail)
    return running


def score_block(rows, row_pos, key_rows, key_pos):
    heads = rows.shape[1] // key_rows.shape[1]
    flat = rows.reshape(rows.shape[0] * heads, key_rows.shape[1])
    raw = lax.dot_general(
        flat, key_rows, (((1,), (1,)), ((), ())), preferred_element_type=jnp.float32
    )
    raw = raw * key_rows.shape[1] ** (-0.5)
    seen = key_pos[None, :] <= jnp.repeat(row_pos, heads)[:, None]
    return jnp.where(seen, raw, jnp.float32(-1e30))


def block_backward(scores, lse, delta, grad_flat, flat_rows, key_rows, value_rows):
    scale = key_rows.shape[1] ** (-0.5)
    prob = jnp.exp(scores - lse[:, None])
    weights = prob.astype(jnp.bfloat16)
    value_part = lax.dot_general(
        weights, grad_flat, (((0,), (0,)), ((), ())), preferred_element_type=jnp.float32
    )
    dprob = lax.dot_general(
        grad_flat, value_rows, (((1,), (1,)), ((), ())), preferred_element_type=jnp.float32
    )
    dscore = (prob * (dprob - delta[:, None])).astype(jnp.bfloat16)
    query_part = jnp.dot(dscore, key_rows, preferred_element_type=jnp.float32) * scale
    key_part = (
        lax.dot_general(
            dscore, flat_rows, (((0,), (0,)), ((), ())), preferred_element_type=jnp.float32
        )
        * scale
    )
    return (query_part, key_part, value_part)


def join_stats(first, second):
    top = jnp.maximum(first[0], second[0])
    total = first[1] * jnp.exp(first[0] - top) + second[1] * jnp.exp(second[0] - top)
    return (top, total)


def block_stats(scores):
    top = jnp.max(scores, axis=1)
    return (top, jnp.sum(jnp.exp(scores - top[:, None]), axis=1))


def lookup(table, wanted):
    slots = jnp.arange(table.shape[0], dtype=jnp.int32)
    return jnp.sum(jnp.where(slots[None, :] == wanted[:, None], table[None, :], 0), axis=1)


def positions(block_order, blocks, tok):
    offsets = jnp.arange(tok, dtype=jnp.int32)
    return (lookup(block_order, blocks)[:, None] * tok + offsets[None, :]).reshape(-1)


def tile_layer(
    row_q,
    col_k,
    col_v,
    row_pos,
    col_pos,
    combine_stats,
    combine_out,
    fetch_grad,
    combine_delta,
    combine_query,
    combine_keys,
):
    width = row_q.shape[1]
    head_dim = col_k.shape[1]
    heads = width // head_dim
    total_rows = row_q.shape[0]
    step_rows = math.gcd(256, total_rows)
    count = total_rows // step_rows
    blocked_q = row_q.reshape(count, step_rows, width)
    blocked_pos = row_pos.reshape(count, step_rows)

    def stats_of(inputs):
        return block_stats(score_block(inputs[0], inputs[1], col_k, col_pos))

    tops, totals = lax.map(stats_of, (blocked_q, blocked_pos))
    tops, totals = combine_stats(tops.reshape(-1), totals.reshape(-1))
    lse = (tops + jnp.log(totals)).reshape(count, step_rows * heads)

    def output_of(inputs):
        scores = score_block(inputs[0], inputs[1], col_k, col_pos)
        weights = jnp.exp(scores - inputs[2][:, None]).astype(jnp.bfloat16)
        return jnp.dot(weights, col_v, preferred_element_type=jnp.float32)

    partial_value = lax.map(output_of, (blocked_q, blocked_pos, lse)).reshape(total_rows, width)
    attended = combine_out(partial_value)
    row_grad = fetch_grad()
    products = jnp.sum(
        row_grad.reshape(-1, head_dim).astype(jnp.float32) * partial_value.reshape(-1, head_dim),
        axis=1,
    )
    delta = combine_delta(products).reshape(count, step_rows * heads)
    blocked_grad = row_grad.reshape(count, step_rows, width)

    def backward_of(carry, inputs):
        rows, pos, lse_part, delta_part, grads = inputs
        scores = score_block(rows, pos, col_k, col_pos)
        query_part, key_part, value_part = block_backward(
            scores,
            lse_part,
            delta_part,
            grads.reshape(-1, head_dim),
            rows.reshape(-1, head_dim),
            col_k,
            col_v,
        )
        return ((carry[0] + key_part, carry[1] + value_part), query_part.reshape(step_rows, width))

    start = (jnp.zeros(col_k.shape, jnp.float32), jnp.zeros(col_k.shape, jnp.float32))
    (key_acc, value_acc), query_parts = lax.scan(
        backward_of, start, (blocked_q, blocked_pos, lse, delta, blocked_grad)
    )
    query_grad = combine_query(query_parts.reshape(total_rows, width))
    key_grad, value_grad = combine_keys(key_acc, value_acc)
    return (attended, query_grad, key_grad, value_grad)


def per_device(queries, keys, values, upstream, block_order):
    tok = queries.shape[0]
    nrow = lax.axis_size("qrow")
    ncol = lax.axis_size("kcol")
    row_idx = lax.axis_index("qrow")
    col_idx = lax.axis_index("kcol")
    row_q = lax.all_gather(queries, "qrow", axis=0, tiled=True)
    col_k, col_v = (
        lax.all_gather(keys, "kcol", axis=0, tiled=True),
        lax.all_gather(values, "kcol", axis=0, tiled=True),
    )
    row_pos = positions(block_order, jnp.arange(nrow, dtype=jnp.int32) * ncol + col_idx, tok)
    col_pos = positions(block_order, row_idx * ncol + jnp.arange(ncol, dtype=jnp.int32), tok)
    attended, query_grad, key_grad, value_grad = tile_layer(
        row_q,
        col_k,
        col_v,
        row_pos,
        col_pos,
        lambda tops, totals: merged((tops, totals), "qrow", join_stats),
        lambda partial_value: lax.psum_scatter(
            partial_value, "qrow", scatter_dimension=0, tiled=True
        ),
        lambda: lax.all_gather(upstream, "qrow", axis=0, tiled=True),
        lambda products: lax.psum(products, "qrow"),
        lambda parts: lax.psum_scatter(parts, "qrow", scatter_dimension=0, tiled=True),
        lambda key_acc, value_acc: (
            lax.psum_scatter(key_acc, "kcol", scatter_dimension=0, tiled=True),
            lax.psum_scatter(value_acc, "kcol", scatter_dimension=0, tiled=True),
        ),
    )
    return (attended, query_grad, key_grad, value_grad)


def solution(mesh):
    return jax.shard_map(
        per_device,
        mesh=mesh,
        in_specs=(
            P(("qrow", "kcol"), None),
            P(("qrow", "kcol"), None),
            P(("qrow", "kcol"), None),
            P(("qrow", "kcol"), None),
            P(),
        ),
        out_specs=(
            P(("qrow", "kcol"), None),
            P(("qrow", "kcol"), None),
            P(("qrow", "kcol"), None),
            P(("qrow", "kcol"), None),
        ),
        check_vma=False,
    )
```

profile of v0, /device:TPU:0, one launch (start us, length us, event | category | flops | bytes accessed | tf_op | source)
XLA Modules:
  0.0 350.2 jit_solution(9840653598324072181)
XLA Ops:
  8.3 10.2 %all_gather.18 = bf16[512,512]{1,0:T(8,128)(2,1)} all-gather(bf16[128,512]{1,0:T(8,128)(2,1)} %param.13), channel_id=1, replica_groups=mesh['qrow'=4,'kcol'=8] {'qrow'}, dimensions={0}, use_global_device_ids=true | all-gather | bytes 655360 | tf_op jit(solution)/shard_map/all_gather | solution.py:143
  18.5 31.4 %all_gather.19 = bf16[1024,128]{1,0:T(8,128)(2,1)S(1)} all-gather(bf16[128,128]{1,0:T(8,128)(2,1)} %param.14), channel_id=1, replica_groups=mesh['qrow'=4,'kcol'=8] {'kcol'}, dimensions={0}, use_global_device_ids=true | all-gather | bytes 294912 | tf_op jit(solution)/shard_map/all_gather | solution.py:145
  50.8 14.9 %while.52 = (s32[]{:T(128)}, f32[2,1024]{1,0:T(2,128)S(1)}, f32[2,1024]{1,0:T(2,128)S(1)}, s32[2,256]{1,0:T(2,128)S(1)}, bf16[2,256,512]{2,1,0:T(8,128)(2,1)}, /...) while((s32[]{:T(128)}, f32[2,1024]{1,0:T(2,128)S(1)}, ...), condition=%wide.region_5.6_spmd.clone, body=%wide.region_2.5_spmd.clone.sunk | while | flops 277871616 | bytes 10026133 | solution.py:95
  52.2 2.7 fusion.58
  54.9 3.2 exponential_reduce_fusion.2
  59.7 2.7 fusion.58
  62.4 3.2 exponential_reduce_fusion.2
  65.7 5.2 %all-gather = f32[4,1,2048]{2,1,0:T(1,128)S(1)} all-gather(f32[1,1,2048]{2,1,0:T(1,128)S(1)} %reshape.99), channel_id=1, replica_groups=mesh['qrow'=4,'kcol'=8] {'qrow'}, dimensions={0}, use_global_device_ids=true | all-gather | bytes 40960 | tf_op jit(solution)/shard_map/all_gather | solution.py:10
  70.9 5.2 %all-gather.1 = f32[4,1,2048]{2,1,0:T(1,128)S(1)} all-gather(f32[1,1,2048]{2,1,0:T(1,128)S(1)} %reshape.101), channel_id=1, replica_groups=mesh['qrow'=4,'kcol'=8] {'qrow'}, dimensions={0}, use_global_device_ids=true | all-gather | bytes 40960 | tf_op jit(solution)/shard_map/all_gather | solution.py:10
  76.4 30.8 %all_gather.22 = bf16[1024,128]{1,0:T(8,128)(2,1)S(1)} all-gather(bf16[128,128]{1,0:T(8,128)(2,1)S(1)} %copy-done.8), channel_id=1, replica_groups=mesh['qrow'=4,'kcol'=8] {'kcol'}, dimensions={0}, use_global_device_ids=true | all-gather | bytes 294912 | tf_op jit(solution)/shard_map/all_gather | solution.py:146
  107.1 5.7 %while.53 = (s32[]{:T(128)}, f32[2,1024,128]{2,1,0:T(8,128)S(1)}, s32[2,256]{1,0:T(2,128)S(1)}, bf16[2,256,512]{2,1,0:T(8,128)(2,1)}, bf16[1024,128]{1,0:T(8,128...) while((s32[]{:T(128)}, f32[2,1024,128]{2,1,0:T(8,128)S(1)}, ...), condition=%wide.region_9.10_spmd.clone, body=%wide.region_8.9_spmd.clone.sunk | while | flops 542114816 | bytes 2399381 | solution.py:104
  113.6 6.9 %all_gather.23 = bf16[512,512]{1,0:T(8,128)(2,1)} all-gather(bf16[128,512]{1,0:T(8,128)(2,1)S(1)} %copy-done.7), channel_id=1, replica_groups=mesh['qrow'=4,'kcol'=8] {'qrow'}, dimensions={0}, use_global_device_ids=true | all-gather | bytes 655360 | tf_op jit(solution)/shard_map/all_gather | solution.py:160
  122.2 7.1 %psum.7 = f32[2,1024]{1,0:T(2,128)S(1)} all-reduce(f32[2,1024]{1,0:T(2,128)S(1)} %multiply_reduce_fusion), channel_id=1, replica_groups=mesh['qrow'=4,'kcol'=8] {'qrow'}, use_global_device_ids=true, to_apply=%region_12.13 | all-reduce | flops 2048 | bytes 16384 | tf_op jit(solution)/shard_map/psum | solution.py:161
  129.3 30.4 %while.54 = (s32[]{:T(128)}, f32[1024,128]{1,0:T(8,128)S(1)}, f32[1024,128]{1,0:T(8,128)}, f32[2,256,512]{2,1,0:T(8,128)}, s32[2,256]{1,0:T(2,128)S(1)}, /*index...) while((s32[]{:T(128)}, f32[1024,128]{1,0:T(8,128)S(1)}, ...), condition=%wide.region_14.15_spmd.clone, body=%wide.region_13.14_spmd.clone.sunk | while | flops 1355547648 | bytes 49610036 | solution.py:129
  130.6 2.6 fusion.73
  134.4 3.7 %multiply_convert_fusion.2 = bf16[1024,1024]{1,0:T(8,128)(2,1)S(1)} fusion(f32[1024,1024]{1,0:T(8,128)} %fusion.73, bf16[1024,128]{1,0:T(8,128)(2,1)} %reshape.122, bf16[1024,128]{1,0:T(8,128)(2,1)} %get-tuple-element.661, f32[1024]{0:T(1024)S(1)} %bitcast.122, f32[1024]{0:T(1024)S(1)} %bitcast.120, s32[1024]{0:T(1024)S(1)} %add_bitcast_fusion.8, ...), kind=kOutput, calls=%fused_computation.22.clone.1 | convolution fusion | flops 275775488 | bytes 6832128 | tf_op jit(solution)/shard_map/while/body/eval_jaxpr/dot_general | solution.py:35
  140.4 1.6 fusion.75
  145.7 2.6 fusion.73
  149.5 3.7 %multiply_convert_fusion.2 = bf16[1024,1024]{1,0:T(8,128)(2,1)S(1)} fusion(f32[1024,1024]{1,0:T(8,128)} %fusion.73, bf16[1024,128]{1,0:T(8,128)(2,1)} %reshape.122, bf16[1024,128]{1,0:T(8,128)(2,1)} %get-tuple-element.661, f32[1024]{0:T(1024)S(1)} %bitcast.122, f32[1024]{0:T(1024)S(1)} %bitcast.120, s32[1024]{0:T(1024)S(1)} %add_bitcast_fusion.8, ...), kind=kOutput, calls=%fused_computation.22.clone.1 | convolution fusion | flops 275775488 | bytes 6832128 | tf_op jit(solution)/shard_map/while/body/eval_jaxpr/dot_general | solution.py:35
  161.3 2.4 reshape.93
  164.2 59.2 %reduce-scatter.9.cloned.1.call-done = f32[128,128]{1,0:T(8,128)} async-done(((f32[1024,128]{1,0:T(8,128)}), f32[128,128]{1,0:T(8,128)}) %reduce-scatter.9.cloned.1.call-update) | async-done | bytes 65552 | tf_op jit(solution)/shard_map/reduce_scatter | solution.py:164
  223.4 65.6 %reduce-scatter.11.cloned.1.call-done = f32[128,128]{1,0:T(8,128)} async-done(((f32[1024,128]{1,0:T(8,128)}), f32[128,128]{1,0:T(8,128)}) %reduce-scatter.11.cloned.1.call-update) | async-done | bytes 65552 | tf_op jit(solution)/shard_map/reduce_scatter | solution.py:165
  289.0 26.9 %reduce-scatter.5.cloned.1.call-done = f32[128,512]{1,0:T(8,128)} async-done(((f32[512,512]{1,0:T(8,128)}), f32[128,512]{1,0:T(8,128)}) %reduce-scatter.5.cloned.1.call-update) | async-done | bytes 262160 | tf_op jit(solution)/shard_map/reduce_scatter | solution.py:157
  315.9 27.8 %reduce-scatter.7.cloned.1.call-done = f32[128,512]{1,0:T(8,128)} async-done(((f32[512,512]{1,0:T(8,128)}), f32[128,512]{1,0:T(8,128)}) %reduce-scatter.7.cloned.1.call-update) | async-done | bytes 262160 | tf_op jit(solution)/shard_map/reduce_scatter | solution.py:162
  (126 shorter events, 31.4 us)
Async XLA Ops:
  7.2 216.3 %reduce-scatter.9.cloned.1.call-start = ((), (), s32[]{:S(2)}) async-start(), calls=%async_computation.6 | async-start | bytes 589824 | tf_op jit(solution)/shard_map/reduce_scatter | solution.py:164
  50.7 25.6 %copy-start.8 = (bf16[128,128]{1,0:T(8,128)(2,1)S(1)}, bf16[128,128]{1,0:T(8,128)(2,1)}, u32[]{:S(2)}) copy-start(bf16[128,128]{1,0:T(8,128)(2,1)} %param.15) | copy-start | bytes 98308
  107.1 6.4 %copy-start.7 = (bf16[128,512]{1,0:T(8,128)(2,1)S(1)}, bf16[128,512]{1,0:T(8,128)(2,1)}, u32[]{:S(2)}) copy-start(bf16[128,512]{1,0:T(8,128)(2,1)} %param.16) | copy-start | bytes 393220
  112.8 0.7 copy-start.6
  113.6 15.7 %copy-start.3 = (f32[2,1024,128]{2,1,0:T(8,128)}, f32[2,1024,128]{2,1,0:T(8,128)S(1)}, u32[]{:S(2)}) copy-start(f32[2,1024,128]{2,1,0:T(8,128)S(1)} %get-tuple-element.180) | copy-start | bytes 3145732
  138.1 1.0 copy-start.2
  138.1 2.3 copy-start
  138.1 2.4 copy-start.4
  142.1 0.8 copy-start.5
  153.2 1.0 copy-start.2
  153.2 2.3 copy-start
  153.2 2.4 copy-start.4
  157.2 0.8 copy-start.5
  159.6 0.8 copy-start.1
  160.5 128.6 %reduce-scatter.11.cloned.1.call-start = ((), (), s32[]{:S(2)}) async-start(), calls=%async_computation.7 | async-start | bytes 589824 | tf_op jit(solution)/shard_map/reduce_scatter | solution.py:165
  161.2 154.7 %reduce-scatter.5.cloned.1.call-start = ((), (), s32[]{:S(2)}) async-start(), calls=%async_computation.4 | async-start | bytes 1310720 | tf_op jit(solution)/shard_map/reduce_scatter | solution.py:157
  163.7 180.0 %reduce-scatter.7.cloned.1.call-start = ((), (), s32[]{:S(2)}) async-start(), calls=%async_computation.5 | async-start | bytes 1310720 | tf_op jit(solution)/shard_map/reduce_scatter | solution.py:162
Sparse Core Ops, SparseCore 0:
  160.6 62.8 reduce-scatter.8
  227.4 61.6 reduce-scatter.10
  292.1 23.7 reduce-scatter.4
  318.9 24.7 reduce-scatter.6
where the time goes:
time: 351 us; the launch traced here: 350 us
  waiting for transfers between devices  181 us (52%)
  blocking collectives  96.8 us (28%)
  matrix products  27.1 us (8%)
  local copies, waits for them, and re-layouts  22.1 us (6%)
  between operations  13.9 us (4%)
  other arithmetic  8.96 us (3%)
    reduce_scatter x1, waiting for transfers between devices, per_device(): lax.psum_scatter(value_acc, 'kcol', scatter_dimension=0, tiled=True)  65.6 us
    reduce_scatter x1, waiting for transfers between devices, per_device(): lax.psum_scatter(key_acc, 'kcol', scatter_dimension=0, tiled=True)  59.2 us
    all_gather x1, blocking collectives, per_device(): lax.all_gather(keys, 'kcol', axis=0, tiled=True)  31.4 us
    all_gather x1, blocking collectives, per_device(): lax.all_gather(values, 'kcol', axis=0, tiled=True)  30.8 us
    reduce_scatter x1, waiting for transfers between devices, per_device(): lax.psum_scatter(parts, 'qrow', scatter_dimension=0, tiled=True)  27.8 us
    reduce_scatter x1, waiting for transfers between devices, per_device(): lax.psum_scatter(partial_value, 'qrow', scatter_dimension=0, tiled=True)  26.9 us
    dot_general x4, matrix products, score_block(): lax.dot_general(flat, key_rows, (((1,), (1,)), ((), ())), preferred_eleme...  10.6 us
    all_gather x2, blocking collectives, merged(): pieces = jax.tree.map(lambda part: lax.all_gather(part, axis), value)  10.4 us
  transfers between devices with their start and end apart: 4, of which 4 were waited for; matrix products, arithmetic and copies ran while one was open for 1% of the time, Pallas kernels for 0%

commit v1 on v0

v1 whole, which is shorter than its diff:
```python
import math

import jax
import jax.numpy as jnp
from jax import lax
from jax.experimental import pallas as pl
from jax.experimental.pallas import tpu as pltpu
from jax.sharding import PartitionSpec as P

AXES = ("qrow", "kcol")
F32, BF16 = jnp.float32, jnp.bfloat16
HIDDEN = 1e30
FLOOR = -1e29
LOG2E = math.log2(math.e)
VMEM = pl.BlockSpec(memory_space=pltpu.VMEM)
SMEM = pl.BlockSpec(memory_space=pltpu.SMEM)


def spread(bits):
    return [
        sum(bit for place, bit in enumerate(bits) if index >> place & 1)
        for index in range(1 << len(bits))
    ]


def swap(value, mask, devices):
    return lax.ppermute(value, AXES, [(i, i ^ mask) for i in range(devices)])


def nt(a, b):
    return lax.dot_general(a, b, (((1,), (1,)), ((), ())), preferred_element_type=F32)


def nn(a, b):
    return lax.dot_general(a, b, (((1,), (0,)), ((), ())), preferred_element_type=F32)


def tn(a, b):
    return lax.dot_general(a, b, (((0,), (0,)), ((), ())), preferred_element_type=F32)


def by_head(ref, dim):
    return jnp.concatenate(
        [ref[:, at : at + dim] for at in range(0, ref.shape[1], dim)], axis=0
    )


def seen_in_block(tok, rows):
    key = lax.broadcasted_iota(jnp.int32, (tok, rows), 0)
    row = lax.broadcasted_iota(jnp.int32, (tok, rows), 1) % tok
    return key <= row


def bias_of(order_ref, row_block, key_block):
    seen = order_ref[key_block] <= order_ref[row_block]
    return jnp.where(seen, jnp.float32(0.0), jnp.float32(HIDDEN))


def forward_kernel(row_masks, key_masks, me_ref, order_ref, *refs):
    nr, nk = len(row_masks), len(key_masks)
    qs, ds, kvs = refs[:nr], refs[nr : 2 * nr], refs[2 * nr : 2 * nr + nk]
    stats_ref, *outs = refs[2 * nr + nk : -1]
    s_ref = refs[-1]
    tok, width = qs[0].shape
    dim = kvs[0].shape[1] // 2
    rows = tok * (width // dim)
    unit = dim**-0.5 * LOG2E
    me = me_ref[0]
    for r in range(nr):
        q = by_head(qs[r], dim)
        top = None
        for j in range(nk):
            s = nt(kvs[j][:, :dim], q) * unit
            if r == 0 and j == 0:
                s = jnp.where(seen_in_block(tok, rows), s, -HIDDEN)
                bias = jnp.float32(0.0)
            else:
                bias = bias_of(order_ref, me ^ row_masks[r], me ^ key_masks[j])
            s_ref[j * tok : (j + 1) * tok, :] = s
            part = jnp.max(s, axis=0, keepdims=True) - bias
            top = part if top is None else jnp.maximum(top, part)
        top = jnp.maximum(top, FLOOR)
        total, acc = None, None
        for j in range(nk):
            if r == 0 and j == 0:
                bias = jnp.float32(0.0)
            else:
                bias = bias_of(order_ref, me ^ row_masks[r], me ^ key_masks[j])
            p = jnp.exp2(s_ref[j * tok : (j + 1) * tok, :] - (top + bias))
            part = jnp.sum(p, axis=0, keepdims=True)
            total = part if total is None else total + part
            out = tn(kvs[j][:, dim:], p.astype(BF16))
            acc = out if acc is None else acc + out
        prods = []
        for h in range(width // dim):
            span = slice(h * tok, (h + 1) * tok)
            piece = acc[:, span]
            grads = ds[r][:, h * dim : (h + 1) * dim].astype(F32).T
            prods.append(jnp.sum(piece * grads, axis=0, keepdims=True))
            outs[r][:, h * dim : (h + 1) * dim] = piece.T.astype(outs[r].dtype)
        stats_ref[4 * r : 4 * r + 1, :] = top
        stats_ref[4 * r + 1 : 4 * r + 2, :] = total
        stats_ref[4 * r + 2 : 4 * r + 3, :] = jnp.concatenate(prods, axis=1)
        stats_ref[4 * r + 3 : 4 * r + 4, :] = jnp.zeros_like(top)


def joined(stats, r):
    tops = [ref[4 * (r ^ a) : 4 * (r ^ a) + 1, :] for a, ref in enumerate(stats)]
    best = tops[0]
    for top in tops[1:]:
        best = jnp.maximum(best, top)
    shares = [jnp.exp2(top - best) for top in tops]
    total = sum(
        share * ref[4 * (r ^ a) + 1 : 4 * (r ^ a) + 2, :]
        for a, (share, ref) in enumerate(zip(shares, stats))
    )
    prods = sum(
        share * ref[4 * (r ^ a) + 2 : 4 * (r ^ a) + 3, :]
        for a, (share, ref) in enumerate(zip(shares, stats))
    )
    inverse = 1.0 / total
    return [share * inverse for share in shares], best + jnp.log2(total), prods * inverse


def backward_kernel(row_masks, key_masks, me_ref, order_ref, *refs):
    nr, nk = len(row_masks), len(key_masks)
    stats = refs[:nr]
    qs, ds, kvs = refs[nr : 2 * nr], refs[2 * nr : 3 * nr], refs[3 * nr : 3 * nr + nk]
    outs = refs[3 * nr + nk : 4 * nr + nk]
    keep_ref, send_ref, acc_ref = refs[4 * nr + nk :]
    tok, width = qs[0].shape
    dim = kvs[0].shape[1] // 2
    rows = tok * (width // dim)
    scale = dim**-0.5
    me = me_ref[0]
    for r in range(nr):
        q, d = by_head(qs[r], dim), by_head(ds[r], dim)
        _, lse, delta = joined(stats, r)
        acc = None
        for j in range(nk):
            k, v = kvs[j][:, :dim], kvs[j][:, dim:]
            s = nt(k, q) * (scale * LOG2E)
            if r == 0 and j == 0:
                p = jnp.where(seen_in_block(tok, rows), jnp.exp2(s - lse), 0.0)
            else:
                p = jnp.exp2(s - (lse + bias_of(order_ref, me ^ row_masks[r], me ^ key_masks[j])))
            t = (p * (nt(v, d) - delta)).astype(BF16)
            span = slice(j * tok, (j + 1) * tok)
            key_part, value_part = nn(t, q), nn(p.astype(BF16), d)
            if r == 0:
                acc_ref[span, :dim] = key_part
                acc_ref[span, dim:] = value_part
            else:
                acc_ref[span, :dim] += key_part
                acc_ref[span, dim:] += value_part
            out = tn(k, t)
            acc = out if acc is None else acc + out
        for h in range(width // dim):
            piece = acc[:, h * tok : (h + 1) * tok].T * scale
            outs[r][:, h * dim : (h + 1) * dim] = piece.astype(outs[r].dtype)
    half = keep_ref.shape[0]
    for ref, at in ((keep_ref, 0), (send_ref, half)):
        ref[:, :dim] = (acc_ref[at : at + half, :dim] * scale).astype(ref.dtype)
        ref[:, dim:] = acc_ref[at : at + half, dim:].astype(ref.dtype)


def pair_kernel(keep_ref, got_ref, own_ref, *sends):
    tok = own_ref.shape[0]
    for i, ref in enumerate((own_ref, *sends)):
        span = slice(i * tok, (i + 1) * tok)
        ref[...] = (keep_ref[span, :] + got_ref[span, :].astype(F32)).astype(ref.dtype)


def sum_kernel(*refs):
    *ins, out = refs
    total = ins[0][...]
    for ref in ins[1:]:
        total += ref[...].astype(F32)
    out[...] = total


def key_sum_kernel(*refs):
    *ins, key_ref, value_ref = refs
    dim = key_ref.shape[1]
    total = ins[0][...]
    for ref in ins[1:]:
        total += ref[...].astype(F32)
    key_ref[...] = total[:, :dim]
    value_ref[...] = total[:, dim:]


def attended_kernel(count, dim, *refs):
    stats, parts, out = refs[:count], refs[count : 2 * count], refs[2 * count]
    tok, width = out.shape
    shares, _, _ = joined(stats, 0)
    for h in range(width // dim):
        total = None
        for a in range(count):
            row = shares[a][:, h * tok : (h + 1) * tok]
            column = jnp.broadcast_to(row, (tok, tok)).T[:, :1]
            part = parts[a][:, h * dim : (h + 1) * dim].astype(F32) * column
            total = part if total is None else total + part
        out[:, h * dim : (h + 1) * dim] = total


def call(kernel, outs, *args, scalars=0, scratch=(), flops=0):
    nbytes = sum(a.size * a.dtype.itemsize for a in (*args, *outs))
    return pl.pallas_call(
        kernel,
        out_shape=outs,
        in_specs=[SMEM] * scalars + [VMEM] * (len(args) - scalars),
        out_specs=[VMEM] * len(outs),
        scratch_shapes=list(scratch),
        cost_estimate=pl.CostEstimate(flops=flops, bytes_accessed=nbytes, transcendentals=0),
    )(*args)


def per_device(queries, keys, values, upstream, block_order):
    tok, width = queries.shape
    dim = keys.shape[1]
    heads = width // dim
    rows = tok * heads
    nrow, ncol = lax.axis_size("qrow"), lax.axis_size("kcol")
    devices = nrow * ncol
    row_bits = [ncol << i for i in range(1, nrow.bit_length() - 1)] + [1]
    far_bits = [1 << i for i in range(1, ncol.bit_length() - 1)]
    pair = ncol
    row_masks = spread(row_bits)
    far_masks = spread(far_bits)
    key_masks = far_masks + [pair | mask for mask in far_masks]
    nr, nf, nk = len(row_masks), len(far_masks), len(key_masks)
    me = (lax.axis_index("qrow") * ncol + lax.axis_index("kcol")).astype(jnp.int32).reshape(1)

    def send(value, mask):
        return swap(value, mask, devices)

    def shape(dims, kind):
        return jax.ShapeDtypeStruct(dims, kind)

    def relayed(value, bits):
        parts = {0: value}
        for bit in bits:
            parts.update({mask | bit: send(part, bit) for mask, part in list(parts.items())})
        return [parts[mask] for mask in row_masks]

    q = relayed(queries, row_bits)
    d = relayed(upstream, row_bits[::-1])
    own = jnp.concatenate([keys, values], axis=1)
    far = [own] + [send(own, mask) for mask in far_masks[1:]]
    kv = far + [send(part, pair) for part in far]

    work = 2 * rows * nr * tok * nk * dim
    stats, *parts = call(
        lambda *refs: forward_kernel(row_masks, key_masks, *refs),
        [shape((4 * nr, rows), F32), shape((tok, width), F32)]
        + [shape((tok, width), BF16)] * (nr - 1),
        me, block_order, *q, *d, *kv,
        scalars=2, scratch=[pltpu.VMEM((nk * tok, rows), F32)], flops=2 * work,
    )
    all_stats = [stats] + [send(stats, mask) for mask in row_masks[1:]]
    all_parts = parts[:1] + [send(p, mask) for p, mask in zip(parts[1:], row_masks[1:])]
    *query_parts, keep, give = call(
        lambda *refs: backward_kernel(row_masks, key_masks, *refs),
        [shape((tok, width), F32)]
        + [shape((tok, width), BF16)] * (nr - 1)
        + [shape((nf * tok, 2 * dim), F32), shape((nf * tok, 2 * dim), BF16)],
        me, block_order, *all_stats, *q, *d, *kv,
        scalars=2, scratch=[pltpu.VMEM((nk * tok, 2 * dim), F32)], flops=5 * work,
    )
    got = send(give, pair)
    own_kv, *far_kv = call(
        pair_kernel,
        [shape((tok, 2 * dim), F32)] + [shape((tok, 2 * dim), BF16)] * (nf - 1),
        keep, got,
    )
    query_in = [send(p, mask) for p, mask in zip(query_parts[1:], row_masks[1:])]
    far_in = [send(p, mask) for p, mask in zip(far_kv, far_masks[1:])]
    (attended,) = call(
        lambda *refs: attended_kernel(nr, dim, *refs),
        [shape((tok, width), F32)], *all_stats, *all_parts,
    )
    (query_grad,) = call(sum_kernel, [shape((tok, width), F32)], query_parts[0], *query_in)
    key_grad, value_grad = call(key_sum_kernel, [shape((tok, dim), F32)] * 2, own_kv, *far_in)
    return attended, query_grad, key_grad, value_grad


def solution(mesh):
    spec = P(AXES, None)
    return jax.shard_map(
        per_device,
        mesh=mesh,
        in_specs=(spec,) * 4 + (P(),),
        out_specs=(spec,) * 4,
        check_vma=False,
    )
```

time: 351 us -> 71.7 us (0.20)
  waiting for transfers between devices: 181 us -> 13.8 us
  blocking collectives: 96.8 us -> 0 us
  starting transfers between devices: 0.16 us -> 28.1 us
  matrix products: 27.1 us -> 0 us
  Pallas kernels: 0 us -> 25.2 us
  local copies, waits for them, and re-layouts: 22.1 us -> 3.36 us
  between operations: 13.9 us -> 0.91 us
  other arithmetic: 8.96 us -> 0 us
    reduce_scatter x4 -> x0, waiting for transfers between devices: 179 us -> none  [the longest x1 65.6 us: per_device(): lax.psum_scatter(value_acc, 'kcol', scatter_dimension=0, tiled=True)]
    all_gather x6 -> x0, blocking collectives: 89.7 us -> none  [the longest x1 31.4 us: per_device(): lax.all_gather(keys, 'kcol', axis=0, tiled=True)]
    ppermute x0 -> x26, starting transfers between devices: none -> 28.1 us  [swap(): return lax.ppermute(value, AXES, [(i, i ^ mask) for i in range(devices)])]
    dot_general x14 -> x0, matrix products: 27.1 us -> none  [the longest x4 10.6 us: score_block(): lax.dot_general(flat, key_rows, (((1,), (1,)), ((), ())), preferred_eleme...]
    pallas_call x0 -> x6, Pallas kernels: none -> 25.2 us  [call(): pl.pallas_call(kernel, out_shape=outs, in_specs=[SMEM] * scalars + [VMEM]...]
    ppermute x0 -> x26, waiting for transfers between devices: none -> 13.8 us  [swap(): return lax.ppermute(value, AXES, [(i, i ^ mask) for i in range(devices)])]
    reduce_sum x5 -> x0, other arithmetic: 8.45 us -> none  [the longest x2 6.42 us: block_stats(): return (top, jnp.sum(jnp.exp(scores - top[:, None]), axis=1))]
    psum x1 -> x0, blocking collectives: 7.1 us -> none  [per_device(): lax.psum(products, 'qrow')]
  transfers between devices with their start and end apart: 4 -> 26, of which waited for: 4 -> 12; matrix products, arithmetic and copies ran while one was open for 1% -> 0% of each run, Pallas kernels for 0% -> 9%
where the time goes in v1:
time: 71.7 us; the launch traced here: 71.4 us
  starting transfers between devices  28.1 us (39%)
  Pallas kernels  25.2 us (35%)
  waiting for transfers between devices  13.8 us (19%)
  local copies, waits for them, and re-layouts  3.36 us (5%)
  between operations  0.91 us (1%)
    ppermute x26, starting transfers between devices, swap(): return lax.ppermute(value, AXES, [(i, i ^ mask) for i in range(devices)])  28.1 us
    pallas_call x6, Pallas kernels, call(): pl.pallas_call(kernel, out_shape=outs, in_specs=[SMEM] * scalars + [VMEM]...  25.2 us
    ppermute x26, waiting for transfers between devices, swap(): return lax.ppermute(value, AXES, [(i, i ^ mask) for i in range(devices)])  13.8 us
    unnamed x63, local copies, waits for them, and re-layouts  3.35 us
  transfers between devices with their start and end apart: 26, of which 12 were waited for; matrix products, arithmetic and copies ran while one was open for 0% of the time, Pallas kernels for 9%

profile of v1, /device:TPU:0, one launch (start us, length us, event | category | flops | bytes accessed | tf_op | source)
XLA Modules:
  0.0 71.4 jit_solution(7911560880646212039)
XLA Ops:
  0.6 0.8 %constant_dynamic-update-slice_fusion.1 = bf16[128,256]{1,0:T(8,128)(2,1)S(1)} fusion(bf16[128,128]{1,0:T(8,128)(2,1)} %param.6), kind=kLoop, calls=%fused_computation.1 | loop fusion | bytes 65536
  1.4 3.1 %collective-permute-start.6 = (bf16[128,256]{1,0:T(8,128)(2,1)S(1)}, bf16[128,256]{1,0:T(8,128)(2,1)S(1)}, u32[]{:S(2)}, u32[]{:S(2)}) collective-permute-start(bf16[128,256]{1,0:T(8,128)(2,1)S(1)} %constant_dynamic-update-slice_fusion.refs_10_.refs_14_), channel_id=1, source_target_pairs={{0,2},{1,3},{2,0},{3,1},{4,6},{5,7},{6,4},{7,5},{8,10},{9,11},{10,... | collective-permute-start | bytes 196616 | tf_op jit(solution)/shard_map/ppermute | solution.py:27
  4.6 2.6 %collective-permute-start.7 = (bf16[128,256]{1,0:T(8,128)(2,1)S(1)}, bf16[128,256]{1,0:T(8,128)(2,1)S(1)}, u32[]{:S(2)}, u32[]{:S(2)}) collective-permute-start(bf16[128,256]{1,0:T(8,128)(2,1)S(1)} %constant_dynamic-update-slice_fusion.refs_10_.refs_14_), channel_id=1, source_target_pairs={{0,4},{1,5},{2,6},{3,7},{4,0},{5,1},{6,2},{7,3},{8,12},{9,13},{10,... | collective-permute-start | bytes 196616 | tf_op jit(solution)/shard_map/ppermute | solution.py:27
  7.2 1.5 %collective-permute-start = (bf16[128,512]{1,0:T(8,128)(2,1)}, bf16[128,512]{1,0:T(8,128)(2,1)S(1)}, u32[]{:S(2)}, u32[]{:S(2)}) collective-permute-start(bf16[128,512]{1,0:T(8,128)(2,1)} %refs_6_.3), channel_id=1, source_target_pairs={{0,16},{1,17},{2,18},{3,19},{4,20},{5,21},{6,22},{7,23},{8,24},{9,... | collective-permute-start | bytes 393224 | tf_op jit(solution)/shard_map/ppermute | solution.py:27
  8.6 1.5 %collective-permute-start.4 = (bf16[128,512]{1,0:T(8,128)(2,1)}, bf16[128,512]{1,0:T(8,128)(2,1)S(1)}, u32[]{:S(2)}, u32[]{:S(2)}) collective-permute-start(bf16[128,512]{1,0:T(8,128)(2,1)} %refs_10_.1), channel_id=1, source_target_pairs={{0,1},{1,0},{2,3},{3,2},{4,5},{5,4},{6,7},{7,6},{8,9},{9,8},{10,11... | collective-permute-start | bytes 393224 | tf_op jit(solution)/shard_map/ppermute | solution.py:27
  10.9 1.1 %collective-permute-start.3 = (bf16[128,512]{1,0:T(8,128)(2,1)}, bf16[128,512]{1,0:T(8,128)(2,1)S(1)}, u32[]{:S(2)}, u32[]{:S(2)}) collective-permute-start(bf16[128,512]{1,0:T(8,128)(2,1)} %refs_10_.1), channel_id=1, source_target_pairs={{0,16},{1,17},{2,18},{3,19},{4,20},{5,21},{6,22},{7,23},{8,24},{9,... | collective-permute-start | bytes 393224 | tf_op jit(solution)/shard_map/ppermute | solution.py:27
  12.0 4.2 %collective-permute-done.8.refs_13_.refs_17_ = bf16[128,256]{1,0:T(8,128)(2,1)S(1)} collective-permute-done((bf16[128,256]{1,0:T(8,128)(2,1)S(1)}, bf16[128,256]{1,0:T(8,128)(2,1)S(1)}, u32[]{:S(2)}, u32[]{:S(2)}) %collective-permute-start.8) | collective-permute-done | bytes 65568 | tf_op jit(solution)/shard_map/ppermute | solution.py:27
  19.3 2.9 %collective-permute-done.2.refs_5_.refs_9_ = bf16[128,512]{1,0:T(8,128)(2,1)S(1)} collective-permute-done((bf16[128,512]{1,0:T(8,128)(2,1)S(1)}, bf16[128,512]{1,0:T(8,128)(2,1)S(1)}, u32[]{:S(2)}, u32[]{:S(2)}) %collective-permute-start.2) | collective-permute-done | bytes 131104 | tf_op jit(solution)/shard_map/ppermute | solution.py:27
  23.0 5.8 %shard_map.84 = (f32[16,512]{1,0:T(8,128)}, f32[128,512]{1,0:T(8,128)}, bf16[128,512]{1,0:T(8,128)(2,1)}, bf16[128,512]{1,0:T(8,128)(2,1)}, bf16[128,512]{1,0:T(8,128)(2,1)}) custom-call(s32[1]{0:T(128)} %bitcast.refs_0_, s32[32]{0:T(128)} %refs_1_.3, bf16[128,512]{1,0:T(8,128)(2,1)} %refs_6_.3, bf16[128,512]{1,0:T(8,128)(2,1)} %copy-done.15, ...), custom_call_target="tpu_custom_call" | custom-call | flops 1073741824 | bytes 2261124 | tf_op jit(solution)/shard_map/pallas_call | solution.py:208
  29.4 1.5 %collective-permute-start.14 = (f32[16,512]{1,0:T(8,128)}, f32[16,512]{1,0:T(8,128)S(1)}, u32[]{:S(2)}, u32[]{:S(2)}) collective-permute-start(f32[16,512]{1,0:T(8,128)} %get-tuple-element.21.refs_0_.refs_2_), channel_id=1, source_target_pairs={{0,1},{1,0},{2,3},{3,2},{4,5},{5,4},{6,7},{7,6},{8,9},{9,8},{10,11... | collective-permute-start | bytes 98312 | tf_op jit(solution)/shard_map/ppermute | solution.py:27
  31.0 1.4 %collective-permute-start.15 = (f32[16,512]{1,0:T(8,128)}, f32[16,512]{1,0:T(8,128)S(1)}, u32[]{:S(2)}, u32[]{:S(2)}) collective-permute-start(f32[16,512]{1,0:T(8,128)} %get-tuple-element.21.refs_0_.refs_2_), channel_id=1, source_target_pairs={{0,17},{1,16},{2,19},{3,18},{4,21},{5,20},{6,23},{7,22},{8,25},{9,... | collective-permute-start | bytes 98312 | tf_op jit(solution)/shard_map/ppermute | solution.py:27
  32.4 0.8 %collective-permute-done.13.refs_1_.refs_3_ = f32[16,512]{1,0:T(8,128)S(1)} collective-permute-done((f32[16,512]{1,0:T(8,128)}, f32[16,512]{1,0:T(8,128)S(1)}, u32[]{:S(2)}, u32[]{:S(2)}) %collective-permute-start.13) | collective-permute-done | bytes 32800 | tf_op jit(solution)/shard_map/ppermute | solution.py:27
  33.9 2.1 %collective-permute-done.15.refs_3_.refs_5_ = f32[16,512]{1,0:T(8,128)S(1)} collective-permute-done((f32[16,512]{1,0:T(8,128)}, f32[16,512]{1,0:T(8,128)S(1)}, u32[]{:S(2)}, u32[]{:S(2)}) %collective-permute-start.15) | collective-permute-done | bytes 32800 | tf_op jit(solution)/shard_map/ppermute | solution.py:27
  36.6 11.5 %shard_map.86 = (f32[128,512]{1,0:T(8,128)}, bf16[128,512]{1,0:T(8,128)(2,1)}, bf16[128,512]{1,0:T(8,128)(2,1)}, bf16[128,512]{1,0:T(8,128)(2,1)}, f32[512,256]{1,0:T(8,128)}, /*index=5*/bf16[512,256]{1,0:T(8,128)(2,1)}) custom-call(s32[1]{0:T(128)} %bitcast.refs_0_, s32[32]{0:T(128)} %refs_1_.3, f32[16,512]{1,0:T(8,128)} %get-tuple-element.21.refs_0_.refs_2_, ...), custom_call_target="tpu_custom_call" | custom-call | flops 2684354560 | bytes 3145860 | tf_op jit(solution)/shard_map/pallas_call | solution.py:208
  48.2 1.5 %collective-permute-start.16 = (bf16[128,512]{1,0:T(8,128)(2,1)S(1)}, bf16[128,512]{1,0:T(8,128)(2,1)S(1)}, u32[]{:S(2)}, u32[]{:S(2)}) collective-permute-start(bf16[128,512]{1,0:T(8,128)(2,1)S(1)} %copy-done.23), channel_id=1, source_target_pairs={{0,16},{1,17},{2,18},{3,19},{4,20},{5,21},{6,22},{7,23},{8,24},{9,... | collective-permute-start | bytes 393224 | tf_op jit(solution)/shard_map/ppermute | solution.py:27
  50.3 1.5 %collective-permute-start.18 = (bf16[128,512]{1,0:T(8,128)(2,1)S(1)}, bf16[128,512]{1,0:T(8,128)(2,1)S(1)}, u32[]{:S(2)}, u32[]{:S(2)}) collective-permute-start(bf16[128,512]{1,0:T(8,128)(2,1)S(1)} %copy-done.21), channel_id=1, source_target_pairs={{0,17},{1,16},{2,19},{3,18},{4,21},{5,20},{6,23},{7,22},{8,25},{9,... | collective-permute-start | bytes 393224 | tf_op jit(solution)/shard_map/ppermute | solution.py:27
  51.8 1.5 %collective-permute-start.19 = (bf16[128,512]{1,0:T(8,128)(2,1)}, bf16[128,512]{1,0:T(8,128)(2,1)S(1)}, u32[]{:S(2)}, u32[]{:S(2)}) collective-permute-start(bf16[128,512]{1,0:T(8,128)(2,1)} %get-tuple-element.27), channel_id=1, source_target_pairs={{0,16},{1,17},{2,18},{3,19},{4,20},{5,21},{6,22},{7,23},{8,24},{9,... | collective-permute-start | bytes 393224 | tf_op jit(solution)/shard_map/ppermute | solution.py:27
  53.2 1.3 %collective-permute-done.16.refs_5_ = bf16[128,512]{1,0:T(8,128)(2,1)S(1)} collective-permute-done((bf16[128,512]{1,0:T(8,128)(2,1)S(1)}, bf16[128,512]{1,0:T(8,128)(2,1)S(1)}, u32[]{:S(2)}, u32[]{:S(2)}) %collective-permute-start.16) | collective-permute-done | bytes 131104 | tf_op jit(solution)/shard_map/ppermute | solution.py:27
  55.0 2.6 %collective-permute-start.21 = (bf16[128,512]{1,0:T(8,128)(2,1)}, bf16[128,512]{1,0:T(8,128)(2,1)S(1)}, u32[]{:S(2)}, u32[]{:S(2)}) collective-permute-start(bf16[128,512]{1,0:T(8,128)(2,1)} %get-tuple-element.29), channel_id=1, source_target_pairs={{0,17},{1,16},{2,19},{3,18},{4,21},{5,20},{6,23},{7,22},{8,25},{9,... | collective-permute-start | bytes 393224 | tf_op jit(solution)/shard_map/ppermute | solution.py:27
  57.6 1.8 %shard_map.88 = (f32[128,256]{1,0:T(8,128)}, bf16[128,256]{1,0:T(8,128)(2,1)}, bf16[128,256]{1,0:T(8,128)(2,1)}, bf16[128,256]{1,0:T(8,128)(2,1)}) custom-call(f32[512,256]{1,0:T(8,128)} %get-tuple-element.30.keep_ref, bf16[512,256]{1,0:T(8,128)(2,1)} %copy-done), custom_call_target="tpu_custom_call" | custom-call | bytes 1114112 | tf_op jit(solution)/shard_map/pallas_call | solution.py:208
  60.4 3.5 %collective-permute-start.25 = (bf16[128,256]{1,0:T(8,128)(2,1)}, bf16[128,256]{1,0:T(8,128)(2,1)S(1)}, u32[]{:S(2)}, u32[]{:S(2)}) collective-permute-start(bf16[128,256]{1,0:T(8,128)(2,1)} %get-tuple-element.35), channel_id=1, source_target_pairs={{0,6},{1,7},{2,4},{3,5},{4,2},{5,3},{6,0},{7,1},{8,14},{9,15},{10,... | collective-permute-start | bytes 196616 | tf_op jit(solution)/shard_map/ppermute | solution.py:27
  63.9 2.6 %shard_map.85 = f32[128,512]{1,0:T(8,128)} custom-call(f32[16,512]{1,0:T(8,128)} %get-tuple-element.21.refs_0_.refs_2_, f32[16,512]{1,0:T(8,128)} %copy-done.10, f32[16,512]{1,0:T(8,128)} %copy-done.11, f32[16,512]{1,0:T(8,128)} %copy-done.12, f32[128,512]{1,0:T(8,128)} %get-tuple-element.22.refs_4_, bf16[128,512]{1,0:T(8,128)(2,1)} %copy-done.4, ...), custom_call_target="tpu_custom_call" | custom-call | bytes 1048576 | tf_op jit(solution)/shard_map/pallas_call | solution.py:208
  67.2 1.9 %shard_map.87 = f32[128,512]{1,0:T(8,128)} custom-call(f32[128,512]{1,0:T(8,128)} %get-tuple-element.26.refs_0_, bf16[128,512]{1,0:T(8,128)(2,1)} %copy-done.1, bf16[128,512]{1,0:T(8,128)(2,1)} %copy-done.2, bf16[128,512]{1,0:T(8,128)(2,1)} %copy-done.3), custom_call_target="tpu_custom_call" | custom-call | bytes 917504 | tf_op jit(solution)/shard_map/pallas_call | solution.py:208
  69.8 1.6 %shard_map.89 = (f32[128,128]{1,0:T(8,128)}, f32[128,128]{1,0:T(8,128)}) custom-call(f32[128,256]{1,0:T(8,128)} %get-tuple-element.32.refs_0_, bf16[128,256]{1,0:T(8,128)(2,1)} %copy-done.7, bf16[128,256]{1,0:T(8,128)(2,1)} %copy-done.8, bf16[128,256]{1,0:T(8,128)(2,1)} %copy-done.9), custom_call_target="tpu_custom_call" | custom-call | bytes 458752 | tf_op jit(solution)/shard_map/pallas_call | solution.py:208
  (98 shorter events, 9.9 us)
Async XLA Ops:
  1.4 8.9 %collective-permute-start.6 = (bf16[128,256]{1,0:T(8,128)(2,1)S(1)}, bf16[128,256]{1,0:T(8,128)(2,1)S(1)}, u32[]{:S(2)}, u32[]{:S(2)}) collective-permute-start(bf16[128,256]{1,0:T(8,128)(2,1)S(1)} %constant_dynamic-update-slice_fusion.refs_10_.refs_14_), channel_id=1, source_target_pairs={{0,2},{1,3},{2,0},{3,1},{4,6},{5,7},{6,4},{7,5},{8,10},{9,11},{10,... | collective-permute-start | bytes 196616 | tf_op jit(solution)/shard_map/ppermute | solution.py:27
  4.6 6.3 %collective-permute-start.7 = (bf16[128,256]{1,0:T(8,128)(2,1)S(1)}, bf16[128,256]{1,0:T(8,128)(2,1)S(1)}, u32[]{:S(2)}, u32[]{:S(2)}) collective-permute-start(bf16[128,256]{1,0:T(8,128)(2,1)S(1)} %constant_dynamic-update-slice_fusion.refs_10_.refs_14_), channel_id=1, source_target_pairs={{0,4},{1,5},{2,6},{3,7},{4,0},{5,1},{6,2},{7,3},{8,12},{9,13},{10,... | collective-permute-start | bytes 196616 | tf_op jit(solution)/shard_map/ppermute | solution.py:27
  7.2 9.1 %collective-permute-start = (bf16[128,512]{1,0:T(8,128)(2,1)}, bf16[128,512]{1,0:T(8,128)(2,1)S(1)}, u32[]{:S(2)}, u32[]{:S(2)}) collective-permute-start(bf16[128,512]{1,0:T(8,128)(2,1)} %refs_6_.3), channel_id=1, source_target_pairs={{0,16},{1,17},{2,18},{3,19},{4,20},{5,21},{6,22},{7,23},{8,24},{9,... | collective-permute-start | bytes 393224 | tf_op jit(solution)/shard_map/ppermute | solution.py:27
  8.6 8.2 %collective-permute-start.4 = (bf16[128,512]{1,0:T(8,128)(2,1)}, bf16[128,512]{1,0:T(8,128)(2,1)S(1)}, u32[]{:S(2)}, u32[]{:S(2)}) collective-permute-start(bf16[128,512]{1,0:T(8,128)(2,1)} %refs_10_.1), channel_id=1, source_target_pairs={{0,1},{1,0},{2,3},{3,2},{4,5},{5,4},{6,7},{7,6},{8,9},{9,8},{10,11... | collective-permute-start | bytes 393224 | tf_op jit(solution)/shard_map/ppermute | solution.py:27
  10.2 6.1 %collective-permute-start.8 = (bf16[128,256]{1,0:T(8,128)(2,1)S(1)}, bf16[128,256]{1,0:T(8,128)(2,1)S(1)}, u32[]{:S(2)}, u32[]{:S(2)}) collective-permute-start(bf16[128,256]{1,0:T(8,128)(2,1)S(1)} %constant_dynamic-update-slice_fusion.refs_10_.refs_14_), channel_id=1, source_target_pairs={{0,6},{1,7},{2,4},{3,5},{4,2},{5,3},{6,0},{7,1},{8,14},{9,15},{10,... | collective-permute-start | bytes 196616 | tf_op jit(solution)/shard_map/ppermute | solution.py:27
  10.4 7.3 %collective-permute-start.1 = (bf16[128,512]{1,0:T(8,128)(2,1)}, bf16[128,512]{1,0:T(8,128)(2,1)S(1)}, u32[]{:S(2)}, u32[]{:S(2)}) collective-permute-start(bf16[128,512]{1,0:T(8,128)(2,1)} %refs_6_.3), channel_id=1, source_target_pairs={{0,1},{1,0},{2,3},{3,2},{4,5},{5,4},{6,7},{7,6},{8,9},{9,8},{10,11... | collective-permute-start | bytes 393224 | tf_op jit(solution)/shard_map/ppermute | solution.py:27
  10.9 7.1 %collective-permute-start.3 = (bf16[128,512]{1,0:T(8,128)(2,1)}, bf16[128,512]{1,0:T(8,128)(2,1)S(1)}, u32[]{:S(2)}, u32[]{:S(2)}) collective-permute-start(bf16[128,512]{1,0:T(8,128)(2,1)} %refs_10_.1), channel_id=1, source_target_pairs={{0,16},{1,17},{2,18},{3,19},{4,20},{5,21},{6,22},{7,23},{8,24},{9,... | collective-permute-start | bytes 393224 | tf_op jit(solution)/shard_map/ppermute | solution.py:27
  16.3 5.9 %collective-permute-start.2 = (bf16[128,512]{1,0:T(8,128)(2,1)S(1)}, bf16[128,512]{1,0:T(8,128)(2,1)S(1)}, u32[]{:S(2)}, u32[]{:S(2)}) collective-permute-start(bf16[128,512]{1,0:T(8,128)(2,1)S(1)} %collective-permute-done.refs_3_.refs_7_), channel_id=1, source_target_pairs={{0,1},{1,0},{2,3},{3,2},{4,5},{5,4},{6,7},{7,6},{8,9},{9,8},{10,11... | collective-permute-start | bytes 393224 | tf_op jit(solution)/shard_map/ppermute | solution.py:27
  16.8 5.6 %collective-permute-start.5 = (bf16[128,512]{1,0:T(8,128)(2,1)S(1)}, bf16[128,512]{1,0:T(8,128)(2,1)S(1)}, u32[]{:S(2)}, u32[]{:S(2)}) collective-permute-start(bf16[128,512]{1,0:T(8,128)(2,1)S(1)} %collective-permute-done.4.refs_8_.refs_12_), channel_id=1, source_target_pairs={{0,16},{1,17},{2,18},{3,19},{4,20},{5,21},{6,22},{7,23},{8,24},{9,... | collective-permute-start | bytes 393224 | tf_op jit(solution)/shard_map/ppermute | solution.py:27
  17.7 1.3 %collective-permute-start.11 = (bf16[128,256]{1,0:T(8,128)(2,1)S(1)}, bf16[128,256]{1,0:T(8,128)(2,1)S(1)}, u32[]{:S(2)}, u32[]{:S(2)}) collective-permute-start(bf16[128,256]{1,0:T(8,128)(2,1)S(1)} %collective-permute-done.7.refs_12_.refs_16_), channel_id=1, source_target_pairs={{0,8},{1,9},{2,10},{3,11},{4,12},{5,13},{6,14},{7,15},{8,0},{9,1},... | collective-permute-start | bytes 196616 | tf_op jit(solution)/shard_map/ppermute | solution.py:27
  18.0 1.3 %collective-permute-start.12 = (bf16[128,256]{1,0:T(8,128)(2,1)S(1)}, bf16[128,256]{1,0:T(8,128)(2,1)S(1)}, u32[]{:S(2)}, u32[]{:S(2)}) collective-permute-start(bf16[128,256]{1,0:T(8,128)(2,1)S(1)} %collective-permute-done.8.refs_13_.refs_17_), channel_id=1, source_target_pairs={{0,8},{1,9},{2,10},{3,11},{4,12},{5,13},{6,14},{7,15},{8,0},{9,1},... | collective-permute-start | bytes 196616 | tf_op jit(solution)/shard_map/ppermute | solution.py:27
  28.8 4.4 %collective-permute-start.13 = (f32[16,512]{1,0:T(8,128)}, f32[16,512]{1,0:T(8,128)S(1)}, u32[]{:S(2)}, u32[]{:S(2)}) collective-permute-start(f32[16,512]{1,0:T(8,128)} %get-tuple-element.21.refs_0_.refs_2_), channel_id=1, source_target_pairs={{0,16},{1,17},{2,18},{3,19},{4,20},{5,21},{6,22},{7,23},{8,24},{9,... | collective-permute-start | bytes 98312 | tf_op jit(solution)/shard_map/ppermute | solution.py:27
  29.4 4.5 %collective-permute-start.14 = (f32[16,512]{1,0:T(8,128)}, f32[16,512]{1,0:T(8,128)S(1)}, u32[]{:S(2)}, u32[]{:S(2)}) collective-permute-start(f32[16,512]{1,0:T(8,128)} %get-tuple-element.21.refs_0_.refs_2_), channel_id=1, source_target_pairs={{0,1},{1,0},{2,3},{3,2},{4,5},{5,4},{6,7},{7,6},{8,9},{9,8},{10,11... | collective-permute-start | bytes 98312 | tf_op jit(solution)/shard_map/ppermute | solution.py:27
  31.0 5.0 %collective-permute-start.15 = (f32[16,512]{1,0:T(8,128)}, f32[16,512]{1,0:T(8,128)S(1)}, u32[]{:S(2)}, u32[]{:S(2)}) collective-permute-start(f32[16,512]{1,0:T(8,128)} %get-tuple-element.21.refs_0_.refs_2_), channel_id=1, source_target_pairs={{0,17},{1,16},{2,19},{3,18},{4,21},{5,20},{6,23},{7,22},{8,25},{9,... | collective-permute-start | bytes 98312 | tf_op jit(solution)/shard_map/ppermute | solution.py:27
  48.1 6.8 %collective-permute-start.22 = (bf16[512,256]{1,0:T(8,128)(2,1)}, bf16[512,256]{1,0:T(8,128)(2,1)S(1)}, u32[]{:S(2)}, u32[]{:S(2)}) collective-permute-start(bf16[512,256]{1,0:T(8,128)(2,1)} %get-tuple-element.31), channel_id=1, source_target_pairs={{0,8},{1,9},{2,10},{3,11},{4,12},{5,13},{6,14},{7,15},{8,0},{9,1},... | collective-permute-start | bytes 786440 | tf_op jit(solution)/shard_map/ppermute | solution.py:27
  48.2 6.3 %collective-permute-start.16 = (bf16[128,512]{1,0:T(8,128)(2,1)S(1)}, bf16[128,512]{1,0:T(8,128)(2,1)S(1)}, u32[]{:S(2)}, u32[]{:S(2)}) collective-permute-start(bf16[128,512]{1,0:T(8,128)(2,1)S(1)} %copy-done.23), channel_id=1, source_target_pairs={{0,16},{1,17},{2,18},{3,19},{4,20},{5,21},{6,22},{7,23},{8,24},{9,... | collective-permute-start | bytes 393224 | tf_op jit(solution)/shard_map/ppermute | solution.py:27
  49.7 9.7 %collective-permute-start.17 = (bf16[128,512]{1,0:T(8,128)(2,1)S(1)}, bf16[128,512]{1,0:T(8,128)(2,1)S(1)}, u32[]{:S(2)}, u32[]{:S(2)}) collective-permute-start(bf16[128,512]{1,0:T(8,128)(2,1)S(1)} %copy-done.22), channel_id=1, source_target_pairs={{0,1},{1,0},{2,3},{3,2},{4,5},{5,4},{6,7},{7,6},{8,9},{9,8},{10,11... | collective-permute-start | bytes 393224 | tf_op jit(solution)/shard_map/ppermute | solution.py:27
  50.3 9.3 %collective-permute-start.18 = (bf16[128,512]{1,0:T(8,128)(2,1)S(1)}, bf16[128,512]{1,0:T(8,128)(2,1)S(1)}, u32[]{:S(2)}, u32[]{:S(2)}) collective-permute-start(bf16[128,512]{1,0:T(8,128)(2,1)S(1)} %copy-done.21), channel_id=1, source_target_pairs={{0,17},{1,16},{2,19},{3,18},{4,21},{5,20},{6,23},{7,22},{8,25},{9,... | collective-permute-start | bytes 393224 | tf_op jit(solution)/shard_map/ppermute | solution.py:27
  51.8 8.7 %collective-permute-start.19 = (bf16[128,512]{1,0:T(8,128)(2,1)}, bf16[128,512]{1,0:T(8,128)(2,1)S(1)}, u32[]{:S(2)}, u32[]{:S(2)}) collective-permute-start(bf16[128,512]{1,0:T(8,128)(2,1)} %get-tuple-element.27), channel_id=1, source_target_pairs={{0,16},{1,17},{2,18},{3,19},{4,20},{5,21},{6,22},{7,23},{8,24},{9,... | collective-permute-start | bytes 393224 | tf_op jit(solution)/shard_map/ppermute | solution.py:27
  54.5 12.0 %collective-permute-start.20 = (bf16[128,512]{1,0:T(8,128)(2,1)}, bf16[128,512]{1,0:T(8,128)(2,1)S(1)}, u32[]{:S(2)}, u32[]{:S(2)}) collective-permute-start(bf16[128,512]{1,0:T(8,128)(2,1)} %get-tuple-element.28), channel_id=1, source_target_pairs={{0,1},{1,0},{2,3},{3,2},{4,5},{5,4},{6,7},{7,6},{8,9},{9,8},{10,11... | collective-permute-start | bytes 393224 | tf_op jit(solution)/shard_map/ppermute | solution.py:27
  55.0 11.5 %collective-permute-start.21 = (bf16[128,512]{1,0:T(8,128)(2,1)}, bf16[128,512]{1,0:T(8,128)(2,1)S(1)}, u32[]{:S(2)}, u32[]{:S(2)}) collective-permute-start(bf16[128,512]{1,0:T(8,128)(2,1)} %get-tuple-element.29), channel_id=1, source_target_pairs={{0,17},{1,16},{2,19},{3,18},{4,21},{5,20},{6,23},{7,22},{8,25},{9,... | collective-permute-start | bytes 393224 | tf_op jit(solution)/shard_map/ppermute | solution.py:27
  59.4 9.7 %collective-permute-start.23 = (bf16[128,256]{1,0:T(8,128)(2,1)}, bf16[128,256]{1,0:T(8,128)(2,1)S(1)}, u32[]{:S(2)}, u32[]{:S(2)}) collective-permute-start(bf16[128,256]{1,0:T(8,128)(2,1)} %get-tuple-element.33), channel_id=1, source_target_pairs={{0,2},{1,3},{2,0},{3,1},{4,6},{5,7},{6,4},{7,5},{8,10},{9,11},{10,... | collective-permute-start | bytes 196616 | tf_op jit(solution)/shard_map/ppermute | solution.py:27
  59.5 9.6 %collective-permute-start.24 = (bf16[128,256]{1,0:T(8,128)(2,1)}, bf16[128,256]{1,0:T(8,128)(2,1)S(1)}, u32[]{:S(2)}, u32[]{:S(2)}) collective-permute-start(bf16[128,256]{1,0:T(8,128)(2,1)} %get-tuple-element.34), channel_id=1, source_target_pairs={{0,4},{1,5},{2,6},{3,7},{4,0},{5,1},{6,2},{7,3},{8,12},{9,13},{10,... | collective-permute-start | bytes 196616 | tf_op jit(solution)/shard_map/ppermute | solution.py:27
  60.4 8.7 %collective-permute-start.25 = (bf16[128,256]{1,0:T(8,128)(2,1)}, bf16[128,256]{1,0:T(8,128)(2,1)S(1)}, u32[]{:S(2)}, u32[]{:S(2)}) collective-permute-start(bf16[128,256]{1,0:T(8,128)(2,1)} %get-tuple-element.35), channel_id=1, source_target_pairs={{0,6},{1,7},{2,4},{3,5},{4,2},{5,3},{6,0},{7,1},{8,14},{9,15},{10,... | collective-permute-start | bytes 196616 | tf_op jit(solution)/shard_map/ppermute | solution.py:27
  (33 other events, 184.5 us)

commit v2 on v1

v2 whole, which is shorter than its diff:
```python
import math

import jax
import jax.numpy as jnp
from jax import lax
from jax.experimental import pallas as pl
from jax.experimental.pallas import tpu as pltpu
from jax.sharding import PartitionSpec as P


AXES = ("qrow", "kcol")
F32, BF16 = jnp.float32, jnp.bfloat16
HIDDEN = 1e30
FLOOR = -1e29
LOG2E = math.log2(math.e)
VMEM = pl.BlockSpec(memory_space=pltpu.VMEM)
SMEM = pl.BlockSpec(memory_space=pltpu.SMEM)


def spread(bits):
    return [
        sum(bit for place, bit in enumerate(bits) if index >> place & 1)
        for index in range(1 << len(bits))
    ]


def swap(value, mask, devices):
    return lax.ppermute(value, AXES, [(i, i ^ mask) for i in range(devices)])


def nt(a, b):
    return lax.dot_general(a, b, (((1,), (1,)), ((), ())), preferred_element_type=F32)


def nn(a, b):
    return lax.dot_general(a, b, (((1,), (0,)), ((), ())), preferred_element_type=F32)


def tn(a, b):
    return lax.dot_general(a, b, (((0,), (0,)), ((), ())), preferred_element_type=F32)


def by_head(ref, dim, start, width):
    return jnp.concatenate(
        [ref[:, at : at + dim].T for at in range(start, start + width, dim)], axis=1
    )


def pieces(value, count):
    parts = []
    for _ in range(count):
        part = value.astype(BF16)
        value = value - part.astype(F32)
        parts.append(part)
    return parts


def seen_in_block(tok, rows):
    key = lax.broadcasted_iota(jnp.int32, (tok, rows), 0)
    row = lax.broadcasted_iota(jnp.int32, (tok, rows), 1) % tok
    return key <= row


def pack_kernel(row_masks, key_masks, me_ref, table_ref, *refs):
    ins, (rows_ref, keys_ref, bias_ref, order_ref, sems) = refs[:4], refs[4:]
    width, dim = ins[0].shape[1], ins[2].shape[1]
    spots = [
        rows_ref.at[:, :width],
        rows_ref.at[:, width:],
        keys_ref.at[:, :dim],
        keys_ref.at[:, dim:],
    ]
    copies = [
        pltpu.make_async_copy(source, spot, sems.at[i])
        for i, (source, spot) in enumerate(zip((table_ref, *ins), (order_ref, *spots)))
    ]
    for copy in copies:
        copy.start()
    copies[0].wait()
    me = me_ref[0]
    lane = lax.broadcasted_iota(jnp.int32, (1, bias_ref.shape[1]), 1)
    for r, row_mask in enumerate(row_masks):
        row = jnp.zeros(lane.shape, F32)
        for j, key_mask in enumerate(key_masks):
            seen = order_ref[me ^ key_mask] <= order_ref[me ^ row_mask]
            row = jnp.where(lane == j, jnp.where(seen, jnp.float32(0.0), jnp.float32(HIDDEN)), row)
        bias_ref[r : r + 1, :] = row
    for copy in copies[1:]:
        copy.wait()


def forward_kernel(nr, nk, bias_ref, *refs):
    qds, kvs = refs[:nr], refs[nr : nr + nk]
    stats_ref, p_ref, qt_ref, dt_ref = refs[nr + nk : nr + nk + 4]
    outs, (kk_ref, v_ref, s_ref) = refs[nr + nk + 4 : -3], refs[-3:]
    tok, width = qds[0].shape[0], qds[0].shape[1] // 2
    dim = kvs[0].shape[1] // 2
    rows = tok * (width // dim)
    unit = dim**-0.5 * LOG2E
    for j, ref in enumerate(kvs):
        span = slice(j * tok, (j + 1) * tok)
        kk_ref[span, :dim] = ref[:, :dim]
        kk_ref[span, dim:] = ref[:, :dim]
        v_ref[span, :] = ref[:, dim:]

    def score(r):
        q = by_head(qds[r], dim, 0, width)
        qt_ref[:, r * rows : (r + 1) * rows] = q
        scaled = jnp.concatenate(pieces(q.astype(F32) * unit, 2), axis=0)
        s_ref[r % 2] = nn(kk_ref[...], scaled)

    score(0)
    for r in range(nr):
        slot, lanes = r % 2, slice(r * rows, (r + 1) * rows)
        biases, top = [], None
        for j in range(nk):
            span = slice(j * tok, (j + 1) * tok)
            s = s_ref[slot, span, :]
            if r == 0 and j == 0:
                s = jnp.where(seen_in_block(tok, rows), s, -HIDDEN)
                s_ref[slot, span, :] = s
            bias = bias_ref[r : r + 1, j : j + 1]
            biases.append(bias)
            part = jnp.max(s, axis=0, keepdims=True) - bias
            top = part if top is None else jnp.maximum(top, part)
        top = jnp.maximum(top, FLOOR)
        if r + 1 < nr:
            score(r + 1)
        total = None
        for j in range(nk):
            span = slice(j * tok, (j + 1) * tok)
            p = jnp.exp2(s_ref[slot, span, :] - (top + biases[j]))
            part = jnp.sum(p, axis=0, keepdims=True)
            total = part if total is None else total + part
            p_ref[span, lanes] = p.astype(BF16)
        d = by_head(qds[r], dim, width, width)
        dt_ref[:, lanes] = d
        out = tn(v_ref[...], p_ref[:, lanes])
        for h in range(width // dim):
            piece = out[:, h * tok : (h + 1) * tok].astype(outs[r].dtype).T
            outs[r][:, h * dim : (h + 1) * dim] = piece
        stats_ref[4 * r : 4 * r + 1, :] = top
        stats_ref[4 * r + 1 : 4 * r + 2, :] = total
        stats_ref[4 * r + 2 : 4 * r + 3, :] = jnp.sum(out * d.astype(F32), axis=0, keepdims=True)
        stats_ref[4 * r + 3 : 4 * r + 4, :] = jnp.zeros_like(top)


def joined(stats, r):
    held = [ref[4 * (r ^ a) : 4 * (r ^ a) + 3, :] for a, ref in enumerate(stats)]
    best = held[0][0:1]
    for part in held[1:]:
        best = jnp.maximum(best, part[0:1])
    shares = [jnp.exp2(part[0:1] - best) for part in held]
    total = sum(share * part[1:2] for share, part in zip(shares, held))
    prods = sum(share * part[2:3] for share, part in zip(shares, held))
    inverse = 1.0 / total
    return [share * inverse for share in shares], prods * inverse


def backward_kernel(nr, nk, *refs):
    p_ref, qt_ref, dt_ref = refs[:3]
    stats, kvs = refs[3 : nr + 3], refs[nr + 3 : nr + nk + 3]
    outs = refs[nr + nk + 3 : 2 * nr + nk + 3]
    keep_ref, send_ref, k_ref, v_ref, da_ref, g_ref, t_ref, acc_ref = refs[2 * nr + nk + 3 :]
    tok, dim = kvs[0].shape[0], kvs[0].shape[1] // 2
    rows = p_ref.shape[1] // nr
    width = rows // tok * dim
    scale = dim**-0.5
    lane = lax.broadcasted_iota(jnp.int32, (tok, dim), 1)
    ones = jnp.where(lane < 3, jnp.float32(1.0), jnp.float32(0.0)).astype(BF16)
    for j, ref in enumerate(kvs):
        span = slice(j * tok, (j + 1) * tok)
        k_ref[span, :] = ref[:, :dim]
        v_ref[span, :dim] = ref[:, dim:]
        v_ref[span, dim:] = ones
    fill = jnp.zeros((dim - 3, rows), BF16)

    def grads(r):
        slot, lanes = r % 2, slice(r * rows, (r + 1) * rows)
        (share, *_), delta = joined(stats, r)
        da_ref[slot, :dim, :] = dt_ref[:, lanes]
        da_ref[slot, dim:, :] = jnp.concatenate(pieces(-delta, 3) + [fill], axis=0)
        g_ref[slot] = nn(v_ref[...], da_ref[slot])
        return share

    share = grads(0)
    for r in range(nr):
        slot, lanes = r % 2, slice(r * rows, (r + 1) * rows)
        after = grads(r + 1) if r + 1 < nr else None
        for j in range(nk):
            span = slice(j * tok, (j + 1) * tok)
            p = p_ref[span, lanes].astype(F32)
            t_ref[slot, span, :] = (p * g_ref[slot, span, :]).astype(BF16)
        value_part = nt((dt_ref[:, lanes].astype(F32) * share).astype(BF16), p_ref[:, lanes])
        key_part = nt((qt_ref[:, lanes].astype(F32) * share).astype(BF16), t_ref[slot])
        if r == 0:
            acc_ref[:dim, :] = key_part
            acc_ref[dim:, :] = value_part
        else:
            acc_ref[:dim, :] += key_part
            acc_ref[dim:, :] += value_part
        query_part = tn(k_ref[...], t_ref[slot]) * (share * scale)
        for h in range(width // dim):
            piece = query_part[:, h * tok : (h + 1) * tok].astype(outs[r].dtype).T
            outs[r][:, h * dim : (h + 1) * dim] = piece
        share = after
    half = nk // 2
    for j in range(nk):
        ref = keep_ref if j < half else send_ref
        span = slice(j % half * tok, (j % half + 1) * tok)
        cols = slice(j * tok, (j + 1) * tok)
        ref[span, :dim] = (acc_ref[:dim, cols] * scale).astype(ref.dtype).T
        ref[span, dim:] = acc_ref[dim:, cols].astype(ref.dtype).T


def attended_kernel(count, dim, *refs):
    stats, parts, out = refs[:count], refs[count : 2 * count], refs[2 * count]
    tok, width = out.shape
    shares, _ = joined(stats, 0)
    for h in range(width // dim):
        total = None
        across = [share[:, h * tok : (h + 1) * tok] for share in shares]
        across += [jnp.zeros_like(across[0])] * (-count % 8)
        columns = jnp.concatenate(across, axis=0).T
        for a in range(count):
            part = parts[a][:, h * dim : (h + 1) * dim].astype(F32) * columns[:, a : a + 1]
            total = part if total is None else total + part
        out[:, h * dim : (h + 1) * dim] = total


def call(kernel, outs, *args, scalars=0, spaces=VMEM, scratch=(), flops=0, room=None):
    nbytes = sum(a.size * a.dtype.itemsize for a in (*args, *outs))
    return pl.pallas_call(
        kernel,
        out_shape=outs,
        in_specs=[SMEM] * scalars + [spaces] * (len(args) - scalars),
        out_specs=[VMEM] * len(outs),
        scratch_shapes=list(scratch),
        compiler_params=pltpu.CompilerParams(vmem_limit_bytes=room) if room else None,
        cost_estimate=pl.CostEstimate(flops=flops, bytes_accessed=nbytes, transcendentals=0),
    )(*args)


def per_device(queries, keys, values, upstream, block_order):
    tok, width = queries.shape
    dim = keys.shape[1]
    heads = width // dim
    rows = tok * heads
    nrow, ncol = lax.axis_size("qrow"), lax.axis_size("kcol")
    devices = nrow * ncol
    row_bits = [ncol << i for i in range(1, nrow.bit_length() - 1)] + [1]
    far_bits = [1 << i for i in range(1, ncol.bit_length() - 1)]
    pair = ncol
    row_masks = spread(row_bits)
    far_masks = spread(far_bits)
    key_masks = far_masks + [pair | mask for mask in far_masks]
    nr, nf, nk = len(row_masks), len(far_masks), len(key_masks)
    me = (lax.axis_index("qrow") * ncol + lax.axis_index("kcol")).astype(jnp.int32).reshape(1)

    def send(value, mask):
        return swap(value, mask, devices)

    def spray(values, masks):
        return [send(v, mask) for v, mask in zip(values, masks[1:])]

    def shape(dims, kind):
        return jax.ShapeDtypeStruct(dims, kind)

    given = (block_order, queries, upstream, keys, values)
    own_rows, own, bias = call(
        lambda *refs: pack_kernel(row_masks, key_masks, *refs),
        [
            shape((tok, 2 * width), BF16),
            shape((tok, 2 * dim), BF16),
            shape((nr, max(128, nk)), F32),
        ],
        me, *[pltpu.with_memory_space_constraint(a, pltpu.HBM) for a in given],
        scalars=1, spaces=pl.BlockSpec(memory_space=pltpu.HBM),
        scratch=[pltpu.SMEM(block_order.shape, jnp.int32), pltpu.SemaphoreType.DMA((5,))],
        room=4 << 20,
    )
    qd = [own_rows] + spray([own_rows] * (nr - 1), row_masks)
    far = [own] + spray([own] * (nf - 1), far_masks)
    kv = far + [send(part, pair) for part in far]

    score = pltpu.VMEM((2, nk * tok, rows), F32)
    narrow, wide = pltpu.VMEM((nk * tok, dim), BF16), pltpu.VMEM((nk * tok, 2 * dim), BF16)
    room = 4 * nk * tok * nr * rows
    work = 2 * rows * nr * tok * nk * dim
    stats, weights, flat_q, flat_d, *parts = call(
        lambda *refs: forward_kernel(nr, nk, *refs),
        [
            shape((4 * nr, rows), F32),
            shape((nk * tok, nr * rows), BF16),
            shape((dim, nr * rows), BF16),
            shape((dim, nr * rows), BF16),
            shape((tok, width), F32),
        ]
        + [shape((tok, width), BF16)] * (nr - 1),
        bias, *qd, *kv,
        scratch=[wide, narrow, score], flops=2 * work, room=room + (6 << 20),
    )
    all_stats = [stats] + spray([stats] * (nr - 1), row_masks)
    all_parts = parts[:1] + spray(parts[1:], row_masks)
    *row_parts, keep, give = call(
        lambda *refs: backward_kernel(nr, nk, *refs),
        [shape((tok, width), F32)]
        + [shape((tok, width), BF16)] * (nr - 1)
        + [shape((nf * tok, 2 * dim), F32), shape((nf * tok, 2 * dim), BF16)],
        weights, flat_q, flat_d, *all_stats, *kv,
        scratch=[
            narrow,
            wide,
            pltpu.VMEM((2, 2 * dim, rows), BF16),
            score,
            pltpu.VMEM((2, nk * tok, rows), BF16),
            pltpu.VMEM((2 * dim, nk * tok), F32),
        ],
        flops=4 * work,
        room=room + (8 << 20),
    )
    got = send(give, pair)
    summed = keep + got.astype(F32)
    own_kv, *far_kv = [summed[i * tok : (i + 1) * tok] for i in range(nf)]
    far_kv = [part.astype(BF16) for part in far_kv]
    rows_in = spray(row_parts[1:], row_masks)
    far_in = spray(far_kv, far_masks)
    (attended,) = call(
        lambda *refs: attended_kernel(nr, dim, *refs),
        [shape((tok, width), F32)], *all_stats, *all_parts,
        room=8 * nr * tok * width + (4 << 20),
    )
    query_grad = row_parts[0] + sum(part.astype(F32) for part in rows_in)
    key_sum = own_kv + sum(part.astype(F32) for part in far_in)
    key_grad, value_grad = key_sum[:, :dim], key_sum[:, dim:]
    return attended, query_grad, key_grad, value_grad


def solution(mesh):
    spec = P(AXES, None)

    return jax.shard_map(
        per_device,
        mesh=mesh,
        in_specs=(spec,) * 4 + (P(),),
        out_specs=(spec,) * 4,
        check_vma=False,
    )
```

time: 71.7 us -> 59.4 us (0.83)
  Pallas kernels: 25.2 us -> 10.5 us
  waiting for transfers between devices: 13.8 us -> 21.6 us
  starting transfers between devices: 28.1 us -> 24.8 us
  local copies, waits for them, and re-layouts: 3.36 us -> 0.67 us
  other arithmetic: 0 us -> 0.87 us
    pallas_call x6 -> x4, Pallas kernels: 25.2 us -> 10.5 us  [call(): pl.pallas_call(kernel, out_shape=outs, in_specs=[SMEM] * scalars + [space...]
    ppermute x26 -> x23, waiting for transfers between devices: 13.8 us -> 21.6 us  [swap(): return lax.ppermute(value, AXES, [(i, i ^ mask) for i in range(devices)])]
    unnamed x63 -> x0, local copies, waits for them, and re-layouts: 3.35 us -> none
    ppermute x26 -> x23, starting transfers between devices: 28.1 us -> 24.8 us  [swap(): return lax.ppermute(value, AXES, [(i, i ^ mask) for i in range(devices)])]
    add x0 -> x2, other arithmetic: none -> 0.79 us  [the longest x1 0.76 us: per_device(): query_grad = row_parts[0] + sum((part.astype(F32) for part in rows_in))]
  transfers between devices with their start and end apart: 26 -> 23, of which waited for: 12 -> 11; matrix products, arithmetic and copies ran while one was open for 0% -> 1% of each run, Pallas kernels for 9% -> 2%
where the time goes in v2:
time: 59.4 us; the launch traced here: 59.2 us
  starting transfers between devices  24.8 us (42%)
  waiting for transfers between devices  21.6 us (36%)
  Pallas kernels  10.5 us (18%)
  other arithmetic  0.87 us (1%)
  between operations  0.71 us (1%)
  local copies, waits for them, and re-layouts  0.67 us (1%)
    ppermute x23, starting transfers between devices, swap(): return lax.ppermute(value, AXES, [(i, i ^ mask) for i in range(devices)])  24.8 us
    ppermute x23, waiting for transfers between devices, swap(): return lax.ppermute(value, AXES, [(i, i ^ mask) for i in range(devices)])  21.6 us
    pallas_call x4, Pallas kernels, call(): pl.pallas_call(kernel, out_shape=outs, in_specs=[SMEM] * scalars + [space...  10.5 us
  transfers between devices with their start and end apart: 23, of which 11 were waited for; matrix products, arithmetic and copies ran while one was open for 1% of the time, Pallas kernels for 2%

profile of v2, /device:TPU:0, one launch (start us, length us, event | category | flops | bytes accessed | tf_op | source)
XLA Modules:
  0.0 59.2 jit_solution(53083851929202166)
XLA Ops:
  0.6 1.0 %shard_map.84 = (bf16[128,1024]{1,0:T(8,128)(2,1)S(1)}, bf16[128,256]{1,0:T(8,128)(2,1)S(1)}, f32[4,128]{1,0:T(4,128)S(1)}) custom-call(s32[1]{0:T(128)} %bitcast.refs_0_, s32[32]{0:T(128)} %refs_1_.1, bf16[128,512]{1,0:T(8,128)(2,1)} %refs_2_.1, bf16[128,512]{1,0:T(8,128)(2,1)} %refs_3_.1, bf16[128,128]{1,0:T(8,128)(2,1)} %refs_4_.1, bf16[128,128]{1,0:T(8,128)(2,1)} %refs_5_.1), custom_call_target="tpu_custom_call" | custom-call | bytes 657540 | tf_op jit(solution)/shard_map/pallas_call | solution.py:233
  1.7 3.1 %collective-permute-start.3 = (bf16[128,256]{1,0:T(8,128)(2,1)S(1)}, bf16[128,256]{1,0:T(8,128)(2,1)S(1)}, u32[]{:S(2)}, u32[]{:S(2)}) collective-permute-start(bf16[128,256]{1,0:T(8,128)(2,1)S(1)} %get-tuple-element.23.refs_5_.refs_7_), channel_id=1, source_target_pairs={{0,2},{1,3},{2,0},{3,1},{4,6},{5,7},{6,4},{7,5},{8,10},{9,11},{10,... | collective-permute-start | bytes 196616 | tf_op jit(solution)/shard_map/ppermute | solution.py:28
  4.8 1.5 %collective-permute-start = (bf16[128,1024]{1,0:T(8,128)(2,1)S(1)}, bf16[128,1024]{1,0:T(8,128)(2,1)S(1)}, u32[]{:S(2)}, u32[]{:S(2)}) collective-permute-start(bf16[128,1024]{1,0:T(8,128)(2,1)S(1)} %get-tuple-element.22.refs_1_), channel_id=1, source_target_pairs={{0,16},{1,17},{2,18},{3,19},{4,20},{5,21},{6,22},{7,23},{8,24},{9,... | collective-permute-start | bytes 786440 | tf_op jit(solution)/shard_map/ppermute | solution.py:28
  6.3 1.5 %collective-permute-start.1 = (bf16[128,1024]{1,0:T(8,128)(2,1)S(1)}, bf16[128,1024]{1,0:T(8,128)(2,1)S(1)}, u32[]{:S(2)}, u32[]{:S(2)}) collective-permute-start(bf16[128,1024]{1,0:T(8,128)(2,1)S(1)} %get-tuple-element.22.refs_1_), channel_id=1, source_target_pairs={{0,1},{1,0},{2,3},{3,2},{4,5},{5,4},{6,7},{7,6},{8,9},{9,8},{10,11... | collective-permute-start | bytes 786440 | tf_op jit(solution)/shard_map/ppermute | solution.py:28
  8.3 2.6 %collective-permute-start.4 = (bf16[128,256]{1,0:T(8,128)(2,1)S(1)}, bf16[128,256]{1,0:T(8,128)(2,1)S(1)}, u32[]{:S(2)}, u32[]{:S(2)}) collective-permute-start(bf16[128,256]{1,0:T(8,128)(2,1)S(1)} %get-tuple-element.23.refs_5_.refs_7_), channel_id=1, source_target_pairs={{0,4},{1,5},{2,6},{3,7},{4,0},{5,1},{6,2},{7,3},{8,12},{9,13},{10,... | collective-permute-start | bytes 196616 | tf_op jit(solution)/shard_map/ppermute | solution.py:28
  11.1 3.5 %collective-permute-done.4.refs_7_.refs_9_ = bf16[128,256]{1,0:T(8,128)(2,1)S(1)} collective-permute-done((bf16[128,256]{1,0:T(8,128)(2,1)S(1)}, bf16[128,256]{1,0:T(8,128)(2,1)S(1)}, u32[]{:S(2)}, u32[]{:S(2)}) %collective-permute-start.4) | collective-permute-done | bytes 65568 | tf_op jit(solution)/shard_map/ppermute | solution.py:28
  14.6 2.3 %collective-permute-done.5.refs_8_.refs_10_ = bf16[128,256]{1,0:T(8,128)(2,1)S(1)} collective-permute-done((bf16[128,256]{1,0:T(8,128)(2,1)S(1)}, bf16[128,256]{1,0:T(8,128)(2,1)S(1)}, u32[]{:S(2)}, u32[]{:S(2)}) %collective-permute-start.5) | collective-permute-done | bytes 65568 | tf_op jit(solution)/shard_map/ppermute | solution.py:28
  18.3 1.1 %collective-permute-done.9.refs_12_.refs_14_ = bf16[128,256]{1,0:T(8,128)(2,1)S(1)} collective-permute-done((bf16[128,256]{1,0:T(8,128)(2,1)S(1)}, bf16[128,256]{1,0:T(8,128)(2,1)S(1)}, u32[]{:S(2)}, u32[]{:S(2)}) %collective-permute-start.9) | collective-permute-done | bytes 65568 | tf_op jit(solution)/shard_map/ppermute | solution.py:28
  19.5 3.5 %shard_map.85 = (f32[16,512]{1,0:T(8,128)S(1)}, bf16[1024,2048]{1,0:T(8,128)(2,1)S(1)}, bf16[128,2048]{1,0:T(8,128)(2,1)S(1)}, bf16[128,2048]{1,0:T(8,128)(2,1)S...) custom-call(f32[4,128]{1,0:T(4,128)S(1)} %get-tuple-element.21.refs_, ...), custom_call_target="tpu_custom_call" | custom-call | flops 1073741824 | bytes 7505920 | tf_op jit(solution)/shard_map/pallas_call | solution.py:233
  23.0 1.6 %collective-permute-start.10 = (f32[16,512]{1,0:T(8,128)S(1)}, f32[16,512]{1,0:T(8,128)S(1)}, u32[]{:S(2)}, u32[]{:S(2)}) collective-permute-start(f32[16,512]{1,0:T(8,128)S(1)} %get-tuple-element.24.refs_0_.refs_3_), channel_id=1, source_target_pairs={{0,16},{1,17},{2,18},{3,19},{4,20},{5,21},{6,22},{7,23},{8,24},{9,... | collective-permute-start | bytes 98312 | tf_op jit(solution)/shard_map/ppermute | solution.py:28
  24.5 1.5 %collective-permute-start.11 = (f32[16,512]{1,0:T(8,128)S(1)}, f32[16,512]{1,0:T(8,128)S(1)}, u32[]{:S(2)}, u32[]{:S(2)}) collective-permute-start(f32[16,512]{1,0:T(8,128)S(1)} %get-tuple-element.24.refs_0_.refs_3_), channel_id=1, source_target_pairs={{0,1},{1,0},{2,3},{3,2},{4,5},{5,4},{6,7},{7,6},{8,9},{9,8},{10,11... | collective-permute-start | bytes 98312 | tf_op jit(solution)/shard_map/ppermute | solution.py:28
  26.9 1.5 %collective-permute-done.11.refs_2_.refs_5_ = f32[16,512]{1,0:T(8,128)S(1)} collective-permute-done((f32[16,512]{1,0:T(8,128)S(1)}, f32[16,512]{1,0:T(8,128)S(1)}, u32[]{:S(2)}, u32[]{:S(2)}) %collective-permute-start.11) | collective-permute-done | bytes 32800 | tf_op jit(solution)/shard_map/ppermute | solution.py:28
  28.4 2.4 %collective-permute-done.12.refs_3_.refs_6_ = f32[16,512]{1,0:T(8,128)S(1)} collective-permute-done((f32[16,512]{1,0:T(8,128)S(1)}, f32[16,512]{1,0:T(8,128)S(1)}, u32[]{:S(2)}, u32[]{:S(2)}) %collective-permute-start.12) | collective-permute-done | bytes 32800 | tf_op jit(solution)/shard_map/ppermute | solution.py:28
  30.9 4.7 %shard_map.87 = (f32[128,512]{1,0:T(8,128)S(1)}, bf16[128,512]{1,0:T(8,128)(2,1)S(1)}, bf16[128,512]{1,0:T(8,128)(2,1)S(1)}, bf16[128,512]{1,0:T(8,128)(2,1)S(1)...) custom-call(bf16[1024,2048]{1,0:T(8,128)(2,1)S(1)} %get-tuple-element.29.refs_0_, ...), custom_call_target="tpu_custom_call" | custom-call | flops 2147483648 | bytes 7340032 | tf_op jit(solution)/shard_map/pallas_call | solution.py:233
  36.7 2.4 %collective-permute-start.15 = (bf16[128,512]{1,0:T(8,128)(2,1)S(1)}, bf16[128,512]{1,0:T(8,128)(2,1)S(1)}, u32[]{:S(2)}, u32[]{:S(2)}) collective-permute-start(bf16[128,512]{1,0:T(8,128)(2,1)S(1)} %get-tuple-element.28), channel_id=1, source_target_pairs={{0,17},{1,16},{2,19},{3,18},{4,21},{5,20},{6,23},{7,22},{8,25},{9,... | collective-permute-start | bytes 393224 | tf_op jit(solution)/shard_map/ppermute | solution.py:28
  39.6 2.4 %collective-permute-done.13.refs_5_ = bf16[128,512]{1,0:T(8,128)(2,1)S(1)} collective-permute-done((bf16[128,512]{1,0:T(8,128)(2,1)S(1)}, bf16[128,512]{1,0:T(8,128)(2,1)S(1)}, u32[]{:S(2)}, u32[]{:S(2)}) %collective-permute-start.13) | collective-permute-done | bytes 131104 | tf_op jit(solution)/shard_map/ppermute | solution.py:28
  42.6 5.0 %collective-permute-done.14.refs_6_ = bf16[128,512]{1,0:T(8,128)(2,1)S(1)} collective-permute-done((bf16[128,512]{1,0:T(8,128)(2,1)S(1)}, bf16[128,512]{1,0:T(8,128)(2,1)S(1)}, u32[]{:S(2)}, u32[]{:S(2)}) %collective-permute-start.14) | collective-permute-done | bytes 131104 | tf_op jit(solution)/shard_map/ppermute | solution.py:28
  47.6 2.1 %collective-permute-start.16 = (bf16[128,512]{1,0:T(8,128)(2,1)S(1)}, bf16[128,512]{1,0:T(8,128)(2,1)S(1)}, u32[]{:S(2)}, u32[]{:S(2)}) collective-permute-start(bf16[128,512]{1,0:T(8,128)(2,1)S(1)} %get-tuple-element.33), channel_id=1, source_target_pairs={{0,16},{1,17},{2,18},{3,19},{4,20},{5,21},{6,22},{7,23},{8,24},{9,... | collective-permute-start | bytes 393224 | tf_op jit(solution)/shard_map/ppermute | solution.py:28
  49.7 1.3 %shard_map.86 = f32[128,512]{1,0:T(8,128)} custom-call(f32[16,512]{1,0:T(8,128)S(1)} %get-tuple-element.24.refs_0_.refs_3_, f32[16,512]{1,0:T(8,128)S(1)} %collective-permute-done.10.refs_1_.refs_4_, f32[16,512]{1,0:T(8,128)S(1)} %collective-permute-done.11.refs_2_.refs_5_, f32[16,512]{1,0:T(8,128)S(1)} %collective-permute-done.12.refs_3_.refs_6_, ...), custom_call_target="tpu_custom_call" | custom-call | bytes 1048576 | tf_op jit(solution)/shard_map/pallas_call | solution.py:233
  51.1 0.9 %collective-permute-start.22 = (bf16[128,256]{1,0:T(8,128)(2,1)S(1)}, bf16[128,256]{1,0:T(8,128)(2,1)S(1)}, u32[]{:S(2)}, u32[]{:S(2)}) collective-permute-start(bf16[128,256]{1,0:T(8,128)(2,1)S(1)} %get-tuple-element.41), channel_id=1, source_target_pairs={{0,6},{1,7},{2,4},{3,5},{4,2},{5,3},{6,0},{7,1},{8,14},{9,15},{10,... | collective-permute-start | bytes 196616 | tf_op jit(solution)/shard_map/ppermute | solution.py:28
  52.2 3.4 %collective-permute-start.20 = (bf16[128,256]{1,0:T(8,128)(2,1)S(1)}, bf16[128,256]{1,0:T(8,128)(2,1)S(1)}, u32[]{:S(2)}, u32[]{:S(2)}) collective-permute-start(bf16[128,256]{1,0:T(8,128)(2,1)S(1)} %get-tuple-element.40), channel_id=1, source_target_pairs={{0,2},{1,3},{2,0},{3,1},{4,6},{5,7},{6,4},{7,5},{8,10},{9,11},{10,... | collective-permute-start | bytes 196616 | tf_op jit(solution)/shard_map/ppermute | solution.py:28
  55.6 0.8 %add_add_fusion = f32[128,512]{1,0:T(8,128)} fusion(f32[128,512]{1,0:T(8,128)S(1)} %get-tuple-element.32, bf16[128,512]{1,0:T(8,128)(2,1)S(1)} %collective-permute-done.18, bf16[128,512]{1,0:T(8,128)(2,1)S(1)} %collective-permute-done.17, bf16[128,512]{1,0:T(8,128)(2,1)S(1)} %collective-permute-done.16), kind=kLoop, calls=%fused_computation.1 | loop fusion | flops 393216 | bytes 917504 | tf_op jit(solution)/shard_map/add | solution.py:333
  56.3 1.0 %collective-permute-done.22 = bf16[128,256]{1,0:T(8,128)(2,1)S(1)} collective-permute-done((bf16[128,256]{1,0:T(8,128)(2,1)S(1)}, bf16[128,256]{1,0:T(8,128)(2,1)S(1)}, u32[]{:S(2)}, u32[]{:S(2)}) %collective-permute-start.22) | collective-permute-done | bytes 65568 | tf_op jit(solution)/shard_map/ppermute | solution.py:28
  57.3 1.2 %collective-permute-done.21 = bf16[128,256]{1,0:T(8,128)(2,1)S(1)} collective-permute-done((bf16[128,256]{1,0:T(8,128)(2,1)S(1)}, bf16[128,256]{1,0:T(8,128)(2,1)S(1)}, u32[]{:S(2)}, u32[]{:S(2)}) %collective-permute-start.21) | collective-permute-done | bytes 65568 | tf_op jit(solution)/shard_map/ppermute | solution.py:28
  (31 shorter events, 6.2 us)
Async XLA Ops:
  1.7 9.2 %collective-permute-start.3 = (bf16[128,256]{1,0:T(8,128)(2,1)S(1)}, bf16[128,256]{1,0:T(8,128)(2,1)S(1)}, u32[]{:S(2)}, u32[]{:S(2)}) collective-permute-start(bf16[128,256]{1,0:T(8,128)(2,1)S(1)} %get-tuple-element.23.refs_5_.refs_7_), channel_id=1, source_target_pairs={{0,2},{1,3},{2,0},{3,1},{4,6},{5,7},{6,4},{7,5},{8,10},{9,11},{10,... | collective-permute-start | bytes 196616 | tf_op jit(solution)/shard_map/ppermute | solution.py:28
  4.8 14.7 %collective-permute-start = (bf16[128,1024]{1,0:T(8,128)(2,1)S(1)}, bf16[128,1024]{1,0:T(8,128)(2,1)S(1)}, u32[]{:S(2)}, u32[]{:S(2)}) collective-permute-start(bf16[128,1024]{1,0:T(8,128)(2,1)S(1)} %get-tuple-element.22.refs_1_), channel_id=1, source_target_pairs={{0,16},{1,17},{2,18},{3,19},{4,20},{5,21},{6,22},{7,23},{8,24},{9,... | collective-permute-start | bytes 786440 | tf_op jit(solution)/shard_map/ppermute | solution.py:28
  6.3 13.2 %collective-permute-start.1 = (bf16[128,1024]{1,0:T(8,128)(2,1)S(1)}, bf16[128,1024]{1,0:T(8,128)(2,1)S(1)}, u32[]{:S(2)}, u32[]{:S(2)}) collective-permute-start(bf16[128,1024]{1,0:T(8,128)(2,1)S(1)} %get-tuple-element.22.refs_1_), channel_id=1, source_target_pairs={{0,1},{1,0},{2,3},{3,2},{4,5},{5,4},{6,7},{7,6},{8,9},{9,8},{10,11... | collective-permute-start | bytes 786440 | tf_op jit(solution)/shard_map/ppermute | solution.py:28
  7.8 11.7 %collective-permute-start.2 = (bf16[128,1024]{1,0:T(8,128)(2,1)S(1)}, bf16[128,1024]{1,0:T(8,128)(2,1)S(1)}, u32[]{:S(2)}, u32[]{:S(2)}) collective-permute-start(bf16[128,1024]{1,0:T(8,128)(2,1)S(1)} %get-tuple-element.22.refs_1_), channel_id=1, source_target_pairs={{0,17},{1,16},{2,19},{3,18},{4,21},{5,20},{6,23},{7,22},{8,25},{9,... | collective-permute-start | bytes 786440 | tf_op jit(solution)/shard_map/ppermute | solution.py:28
  8.3 6.3 %collective-permute-start.4 = (bf16[128,256]{1,0:T(8,128)(2,1)S(1)}, bf16[128,256]{1,0:T(8,128)(2,1)S(1)}, u32[]{:S(2)}, u32[]{:S(2)}) collective-permute-start(bf16[128,256]{1,0:T(8,128)(2,1)S(1)} %get-tuple-element.23.refs_5_.refs_7_), channel_id=1, source_target_pairs={{0,4},{1,5},{2,6},{3,7},{4,0},{5,1},{6,2},{7,3},{8,12},{9,13},{10,... | collective-permute-start | bytes 196616 | tf_op jit(solution)/shard_map/ppermute | solution.py:28
  10.9 6.1 %collective-permute-start.5 = (bf16[128,256]{1,0:T(8,128)(2,1)S(1)}, bf16[128,256]{1,0:T(8,128)(2,1)S(1)}, u32[]{:S(2)}, u32[]{:S(2)}) collective-permute-start(bf16[128,256]{1,0:T(8,128)(2,1)S(1)} %get-tuple-element.23.refs_5_.refs_7_), channel_id=1, source_target_pairs={{0,6},{1,7},{2,4},{3,5},{4,2},{5,3},{6,0},{7,1},{8,14},{9,15},{10,... | collective-permute-start | bytes 196616 | tf_op jit(solution)/shard_map/ppermute | solution.py:28
  14.6 2.3 %collective-permute-start.6 = (bf16[128,256]{1,0:T(8,128)(2,1)S(1)}, bf16[128,256]{1,0:T(8,128)(2,1)S(1)}, u32[]{:S(2)}, u32[]{:S(2)}) collective-permute-start(bf16[128,256]{1,0:T(8,128)(2,1)S(1)} %get-tuple-element.23.refs_5_.refs_7_), channel_id=1, source_target_pairs={{0,8},{1,9},{2,10},{3,11},{4,12},{5,13},{6,14},{7,15},{8,0},{9,1},... | collective-permute-start | bytes 196616 | tf_op jit(solution)/shard_map/ppermute | solution.py:28
  16.9 1.3 %collective-permute-start.7 = (bf16[128,256]{1,0:T(8,128)(2,1)S(1)}, bf16[128,256]{1,0:T(8,128)(2,1)S(1)}, u32[]{:S(2)}, u32[]{:S(2)}) collective-permute-start(bf16[128,256]{1,0:T(8,128)(2,1)S(1)} %collective-permute-done.3.refs_6_.refs_8_), channel_id=1, source_target_pairs={{0,8},{1,9},{2,10},{3,11},{4,12},{5,13},{6,14},{7,15},{8,0},{9,1},... | collective-permute-start | bytes 196616 | tf_op jit(solution)/shard_map/ppermute | solution.py:28
  16.9 1.4 %collective-permute-start.8 = (bf16[128,256]{1,0:T(8,128)(2,1)S(1)}, bf16[128,256]{1,0:T(8,128)(2,1)S(1)}, u32[]{:S(2)}, u32[]{:S(2)}) collective-permute-start(bf16[128,256]{1,0:T(8,128)(2,1)S(1)} %collective-permute-done.4.refs_7_.refs_9_), channel_id=1, source_target_pairs={{0,8},{1,9},{2,10},{3,11},{4,12},{5,13},{6,14},{7,15},{8,0},{9,1},... | collective-permute-start | bytes 196616 | tf_op jit(solution)/shard_map/ppermute | solution.py:28
  18.2 1.3 %collective-permute-start.9 = (bf16[128,256]{1,0:T(8,128)(2,1)S(1)}, bf16[128,256]{1,0:T(8,128)(2,1)S(1)}, u32[]{:S(2)}, u32[]{:S(2)}) collective-permute-start(bf16[128,256]{1,0:T(8,128)(2,1)S(1)} %collective-permute-done.5.refs_8_.refs_10_), channel_id=1, source_target_pairs={{0,8},{1,9},{2,10},{3,11},{4,12},{5,13},{6,14},{7,15},{8,0},{9,1},... | collective-permute-start | bytes 196616 | tf_op jit(solution)/shard_map/ppermute | solution.py:28
  23.0 4.0 %collective-permute-start.10 = (f32[16,512]{1,0:T(8,128)S(1)}, f32[16,512]{1,0:T(8,128)S(1)}, u32[]{:S(2)}, u32[]{:S(2)}) collective-permute-start(f32[16,512]{1,0:T(8,128)S(1)} %get-tuple-element.24.refs_0_.refs_3_), channel_id=1, source_target_pairs={{0,16},{1,17},{2,18},{3,19},{4,20},{5,21},{6,22},{7,23},{8,24},{9,... | collective-permute-start | bytes 98312 | tf_op jit(solution)/shard_map/ppermute | solution.py:28
  24.5 3.9 %collective-permute-start.11 = (f32[16,512]{1,0:T(8,128)S(1)}, f32[16,512]{1,0:T(8,128)S(1)}, u32[]{:S(2)}, u32[]{:S(2)}) collective-permute-start(f32[16,512]{1,0:T(8,128)S(1)} %get-tuple-element.24.refs_0_.refs_3_), channel_id=1, source_target_pairs={{0,1},{1,0},{2,3},{3,2},{4,5},{5,4},{6,7},{7,6},{8,9},{9,8},{10,11... | collective-permute-start | bytes 98312 | tf_op jit(solution)/shard_map/ppermute | solution.py:28
  26.0 4.8 %collective-permute-start.12 = (f32[16,512]{1,0:T(8,128)S(1)}, f32[16,512]{1,0:T(8,128)S(1)}, u32[]{:S(2)}, u32[]{:S(2)}) collective-permute-start(f32[16,512]{1,0:T(8,128)S(1)} %get-tuple-element.24.refs_0_.refs_3_), channel_id=1, source_target_pairs={{0,17},{1,16},{2,19},{3,18},{4,21},{5,20},{6,23},{7,22},{8,25},{9,... | collective-permute-start | bytes 98312 | tf_op jit(solution)/shard_map/ppermute | solution.py:28
  35.5 15.5 %collective-permute-start.19 = (bf16[512,256]{1,0:T(8,128)(2,1)S(1)}, bf16[512,256]{1,0:T(8,128)(2,1)S(1)}, u32[]{:S(2)}, u32[]{:S(2)}) collective-permute-start(bf16[512,256]{1,0:T(8,128)(2,1)S(1)} %get-tuple-element.37), channel_id=1, source_target_pairs={{0,8},{1,9},{2,10},{3,11},{4,12},{5,13},{6,14},{7,15},{8,0},{9,1},... | collective-permute-start | bytes 786440 | tf_op jit(solution)/shard_map/ppermute | solution.py:28
  35.6 6.4 %collective-permute-start.13 = (bf16[128,512]{1,0:T(8,128)(2,1)S(1)}, bf16[128,512]{1,0:T(8,128)(2,1)S(1)}, u32[]{:S(2)}, u32[]{:S(2)}) collective-permute-start(bf16[128,512]{1,0:T(8,128)(2,1)S(1)} %get-tuple-element.26), channel_id=1, source_target_pairs={{0,16},{1,17},{2,18},{3,19},{4,20},{5,21},{6,22},{7,23},{8,24},{9,... | collective-permute-start | bytes 393224 | tf_op jit(solution)/shard_map/ppermute | solution.py:28
  36.2 11.3 %collective-permute-start.14 = (bf16[128,512]{1,0:T(8,128)(2,1)S(1)}, bf16[128,512]{1,0:T(8,128)(2,1)S(1)}, u32[]{:S(2)}, u32[]{:S(2)}) collective-permute-start(bf16[128,512]{1,0:T(8,128)(2,1)S(1)} %get-tuple-element.27), channel_id=1, source_target_pairs={{0,1},{1,0},{2,3},{3,2},{4,5},{5,4},{6,7},{7,6},{8,9},{9,8},{10,11... | collective-permute-start | bytes 393224 | tf_op jit(solution)/shard_map/ppermute | solution.py:28
  36.7 13.0 %collective-permute-start.15 = (bf16[128,512]{1,0:T(8,128)(2,1)S(1)}, bf16[128,512]{1,0:T(8,128)(2,1)S(1)}, u32[]{:S(2)}, u32[]{:S(2)}) collective-permute-start(bf16[128,512]{1,0:T(8,128)(2,1)S(1)} %get-tuple-element.28), channel_id=1, source_target_pairs={{0,17},{1,16},{2,19},{3,18},{4,21},{5,20},{6,23},{7,22},{8,25},{9,... | collective-permute-start | bytes 393224 | tf_op jit(solution)/shard_map/ppermute | solution.py:28
  39.2 13.0 %collective-permute-start.18 = (bf16[128,512]{1,0:T(8,128)(2,1)S(1)}, bf16[128,512]{1,0:T(8,128)(2,1)S(1)}, u32[]{:S(2)}, u32[]{:S(2)}) collective-permute-start(bf16[128,512]{1,0:T(8,128)(2,1)S(1)} %get-tuple-element.35), channel_id=1, source_target_pairs={{0,17},{1,16},{2,19},{3,18},{4,21},{5,20},{6,23},{7,22},{8,25},{9,... | collective-permute-start | bytes 393224 | tf_op jit(solution)/shard_map/ppermute | solution.py:28
  42.0 13.5 %collective-permute-start.17 = (bf16[128,512]{1,0:T(8,128)(2,1)S(1)}, bf16[128,512]{1,0:T(8,128)(2,1)S(1)}, u32[]{:S(2)}, u32[]{:S(2)}) collective-permute-start(bf16[128,512]{1,0:T(8,128)(2,1)S(1)} %get-tuple-element.34), channel_id=1, source_target_pairs={{0,1},{1,0},{2,3},{3,2},{4,5},{5,4},{6,7},{7,6},{8,9},{9,8},{10,11... | collective-permute-start | bytes 393224 | tf_op jit(solution)/shard_map/ppermute | solution.py:28
  47.6 8.0 %collective-permute-start.16 = (bf16[128,512]{1,0:T(8,128)(2,1)S(1)}, bf16[128,512]{1,0:T(8,128)(2,1)S(1)}, u32[]{:S(2)}, u32[]{:S(2)}) collective-permute-start(bf16[128,512]{1,0:T(8,128)(2,1)S(1)} %get-tuple-element.33), channel_id=1, source_target_pairs={{0,16},{1,17},{2,18},{3,19},{4,20},{5,21},{6,22},{7,23},{8,24},{9,... | collective-permute-start | bytes 393224 | tf_op jit(solution)/shard_map/ppermute | solution.py:28
  51.1 6.3 %collective-permute-start.22 = (bf16[128,256]{1,0:T(8,128)(2,1)S(1)}, bf16[128,256]{1,0:T(8,128)(2,1)S(1)}, u32[]{:S(2)}, u32[]{:S(2)}) collective-permute-start(bf16[128,256]{1,0:T(8,128)(2,1)S(1)} %get-tuple-element.41), channel_id=1, source_target_pairs={{0,6},{1,7},{2,4},{3,5},{4,2},{5,3},{6,0},{7,1},{8,14},{9,15},{10,... | collective-permute-start | bytes 196616 | tf_op jit(solution)/shard_map/ppermute | solution.py:28
  51.9 6.6 %collective-permute-start.21 = (bf16[128,256]{1,0:T(8,128)(2,1)S(1)}, bf16[128,256]{1,0:T(8,128)(2,1)S(1)}, u32[]{:S(2)}, u32[]{:S(2)}) collective-permute-start(bf16[128,256]{1,0:T(8,128)(2,1)S(1)} %get-tuple-element.42), channel_id=1, source_target_pairs={{0,4},{1,5},{2,6},{3,7},{4,0},{5,1},{6,2},{7,3},{8,12},{9,13},{10,... | collective-permute-start | bytes 196616 | tf_op jit(solution)/shard_map/ppermute | solution.py:28
  52.2 6.4 %collective-permute-start.20 = (bf16[128,256]{1,0:T(8,128)(2,1)S(1)}, bf16[128,256]{1,0:T(8,128)(2,1)S(1)}, u32[]{:S(2)}, u32[]{:S(2)}) collective-permute-start(bf16[128,256]{1,0:T(8,128)(2,1)S(1)} %get-tuple-element.40), channel_id=1, source_target_pairs={{0,2},{1,3},{2,0},{3,1},{4,6},{5,7},{6,4},{7,5},{8,10},{9,11},{10,... | collective-permute-start | bytes 196616 | tf_op jit(solution)/shard_map/ppermute | solution.py:28

commit v3 on v2

--- a/solution.py
+++ b/solution.py
@@ -26,10 +26,6 @@
 
 def swap(value, mask, devices):
     return lax.ppermute(value, AXES, [(i, i ^ mask) for i in range(devices)])
-
-
-def nt(a, b):
-    return lax.dot_general(a, b, (((1,), (1,)), ((), ())), preferred_element_type=F32)
 
 
 def nn(a, b):
@@ -191,14 +187,14 @@
             span = slice(j * tok, (j + 1) * tok)
             p = p_ref[span, lanes].astype(F32)
             t_ref[slot, span, :] = (p * g_ref[slot, span, :]).astype(BF16)
-        value_part = nt((dt_ref[:, lanes].astype(F32) * share).astype(BF16), p_ref[:, lanes])
-        key_part = nt((qt_ref[:, lanes].astype(F32) * share).astype(BF16), t_ref[slot])
+        value_part = nn(p_ref[:, lanes], (dt_ref[:, lanes].astype(F32) * share).astype(BF16).T)
+        key_part = nn(t_ref[slot], (qt_ref[:, lanes].astype(F32) * share).astype(BF16).T)
         if r == 0:
-            acc_ref[:dim, :] = key_part
-            acc_ref[dim:, :] = value_part
+            acc_ref[:, :dim] = key_part
+            acc_ref[:, dim:] = value_part
         else:
-            acc_ref[:dim, :] += key_part
-            acc_ref[dim:, :] += value_part
+            acc_ref[:, :dim] += key_part
+            acc_ref[:, dim:] += value_part
         query_part = tn(k_ref[...], t_ref[slot]) * (share * scale)
         for h in range(width // dim):
             piece = query_part[:, h * tok : (h + 1) * tok].astype(outs[r].dtype).T
@@ -209,8 +205,8 @@
         ref = keep_ref if j < half else send_ref
         span = slice(j % half * tok, (j % half + 1) * tok)
         cols = slice(j * tok, (j + 1) * tok)
-        ref[span, :dim] = (acc_ref[:dim, cols] * scale).astype(ref.dtype).T
-        ref[span, dim:] = acc_ref[dim:, cols].astype(ref.dtype).T
+        ref[span, :dim] = (acc_ref[cols, :dim] * scale).astype(ref.dtype)
+        ref[span, dim:] = acc_ref[cols, dim:].astype(ref.dtype)
 
 
 def attended_kernel(count, dim, *refs):
@@ -314,7 +310,7 @@
             pltpu.VMEM((2, 2 * dim, rows), BF16),
             score,
             pltpu.VMEM((2, nk * tok, rows), BF16),
-            pltpu.VMEM((2 * dim, nk * tok), F32),
+            pltpu.VMEM((nk * tok, 2 * dim), F32),
         ],
         flops=4 * work,
         room=room + (8 << 20),

time: 59.4 us -> 58.9 us (level)
  no operation moved by 1% of the time
where the time goes in v3:
time: 58.9 us; the launch traced here: 58.7 us
  starting transfers between devices  24.8 us (42%)
  waiting for transfers between devices  21.6 us (37%)
  Pallas kernels  10.1 us (17%)
  other arithmetic  0.87 us (1%)
  between operations  0.71 us (1%)
  local copies, waits for them, and re-layouts  0.67 us (1%)
    ppermute x23, starting transfers between devices, swap(): return lax.ppermute(value, AXES, [(i, i ^ mask) for i in range(devices)])  24.8 us
    ppermute x23, waiting for transfers between devices, swap(): return lax.ppermute(value, AXES, [(i, i ^ mask) for i in range(devices)])  21.6 us
    pallas_call x4, Pallas kernels, call(): pl.pallas_call(kernel, out_shape=outs, in_specs=[SMEM] * scalars + [space...  10.1 us
  transfers between devices with their start and end apart: 23, of which 11 were waited for; matrix products, arithmetic and copies ran while one was open for 1% of the time, Pallas kernels for 2%

profile of v3, /device:TPU:0, one launch (start us, length us, event | category | flops | bytes accessed | tf_op | source)
XLA Modules:
  0.0 58.7 jit_solution(2577588809358737690)
XLA Ops:
  0.6 1.0 %shard_map.84 = (bf16[128,1024]{1,0:T(8,128)(2,1)S(1)}, bf16[128,256]{1,0:T(8,128)(2,1)S(1)}, f32[4,128]{1,0:T(4,128)S(1)}) custom-call(s32[1]{0:T(128)} %bitcast.refs_0_, s32[32]{0:T(128)} %refs_1_.1, bf16[128,512]{1,0:T(8,128)(2,1)} %refs_2_.1, bf16[128,512]{1,0:T(8,128)(2,1)} %refs_3_.1, bf16[128,128]{1,0:T(8,128)(2,1)} %refs_4_.1, bf16[128,128]{1,0:T(8,128)(2,1)} %refs_5_.1), custom_call_target="tpu_custom_call" | custom-call | bytes 657540 | tf_op jit(solution)/shard_map/pallas_call | solution.py:229
  1.7 3.1 %collective-permute-start.3 = (bf16[128,256]{1,0:T(8,128)(2,1)S(1)}, bf16[128,256]{1,0:T(8,128)(2,1)S(1)}, u32[]{:S(2)}, u32[]{:S(2)}) collective-permute-start(bf16[128,256]{1,0:T(8,128)(2,1)S(1)} %get-tuple-element.23.refs_5_.refs_7_), channel_id=1, source_target_pairs={{0,2},{1,3},{2,0},{3,1},{4,6},{5,7},{6,4},{7,5},{8,10},{9,11},{10,... | collective-permute-start | bytes 196616 | tf_op jit(solution)/shard_map/ppermute | solution.py:28
  4.8 1.5 %collective-permute-start = (bf16[128,1024]{1,0:T(8,128)(2,1)S(1)}, bf16[128,1024]{1,0:T(8,128)(2,1)S(1)}, u32[]{:S(2)}, u32[]{:S(2)}) collective-permute-start(bf16[128,1024]{1,0:T(8,128)(2,1)S(1)} %get-tuple-element.22.refs_1_), channel_id=1, source_target_pairs={{0,16},{1,17},{2,18},{3,19},{4,20},{5,21},{6,22},{7,23},{8,24},{9,... | collective-permute-start | bytes 786440 | tf_op jit(solution)/shard_map/ppermute | solution.py:28
  6.3 1.5 %collective-permute-start.1 = (bf16[128,1024]{1,0:T(8,128)(2,1)S(1)}, bf16[128,1024]{1,0:T(8,128)(2,1)S(1)}, u32[]{:S(2)}, u32[]{:S(2)}) collective-permute-start(bf16[128,1024]{1,0:T(8,128)(2,1)S(1)} %get-tuple-element.22.refs_1_), channel_id=1, source_target_pairs={{0,1},{1,0},{2,3},{3,2},{4,5},{5,4},{6,7},{7,6},{8,9},{9,8},{10,11... | collective-permute-start | bytes 786440 | tf_op jit(solution)/shard_map/ppermute | solution.py:28
  8.3 2.6 %collective-permute-start.4 = (bf16[128,256]{1,0:T(8,128)(2,1)S(1)}, bf16[128,256]{1,0:T(8,128)(2,1)S(1)}, u32[]{:S(2)}, u32[]{:S(2)}) collective-permute-start(bf16[128,256]{1,0:T(8,128)(2,1)S(1)} %get-tuple-element.23.refs_5_.refs_7_), channel_id=1, source_target_pairs={{0,4},{1,5},{2,6},{3,7},{4,0},{5,1},{6,2},{7,3},{8,12},{9,13},{10,... | collective-permute-start | bytes 196616 | tf_op jit(solution)/shard_map/ppermute | solution.py:28
  11.1 3.5 %collective-permute-done.4.refs_7_.refs_9_ = bf16[128,256]{1,0:T(8,128)(2,1)S(1)} collective-permute-done((bf16[128,256]{1,0:T(8,128)(2,1)S(1)}, bf16[128,256]{1,0:T(8,128)(2,1)S(1)}, u32[]{:S(2)}, u32[]{:S(2)}) %collective-permute-start.4) | collective-permute-done | bytes 65568 | tf_op jit(solution)/shard_map/ppermute | solution.py:28
  14.6 2.3 %collective-permute-done.5.refs_8_.refs_10_ = bf16[128,256]{1,0:T(8,128)(2,1)S(1)} collective-permute-done((bf16[128,256]{1,0:T(8,128)(2,1)S(1)}, bf16[128,256]{1,0:T(8,128)(2,1)S(1)}, u32[]{:S(2)}, u32[]{:S(2)}) %collective-permute-start.5) | collective-permute-done | bytes 65568 | tf_op jit(solution)/shard_map/ppermute | solution.py:28
  18.3 1.1 %collective-permute-done.9.refs_12_.refs_14_ = bf16[128,256]{1,0:T(8,128)(2,1)S(1)} collective-permute-done((bf16[128,256]{1,0:T(8,128)(2,1)S(1)}, bf16[128,256]{1,0:T(8,128)(2,1)S(1)}, u32[]{:S(2)}, u32[]{:S(2)}) %collective-permute-start.9) | collective-permute-done | bytes 65568 | tf_op jit(solution)/shard_map/ppermute | solution.py:28
  19.5 3.5 %shard_map.85 = (f32[16,512]{1,0:T(8,128)S(1)}, bf16[1024,2048]{1,0:T(8,128)(2,1)S(1)}, bf16[128,2048]{1,0:T(8,128)(2,1)S(1)}, bf16[128,2048]{1,0:T(8,128)(2,1)S...) custom-call(f32[4,128]{1,0:T(4,128)S(1)} %get-tuple-element.21.refs_, ...), custom_call_target="tpu_custom_call" | custom-call | flops 1073741824 | bytes 7505920 | tf_op jit(solution)/shard_map/pallas_call | solution.py:229
  23.0 1.6 %collective-permute-start.10 = (f32[16,512]{1,0:T(8,128)S(1)}, f32[16,512]{1,0:T(8,128)S(1)}, u32[]{:S(2)}, u32[]{:S(2)}) collective-permute-start(f32[16,512]{1,0:T(8,128)S(1)} %get-tuple-element.24.refs_0_.refs_3_), channel_id=1, source_target_pairs={{0,16},{1,17},{2,18},{3,19},{4,20},{5,21},{6,22},{7,23},{8,24},{9,... | collective-permute-start | bytes 98312 | tf_op jit(solution)/shard_map/ppermute | solution.py:28
  24.5 1.5 %collective-permute-start.11 = (f32[16,512]{1,0:T(8,128)S(1)}, f32[16,512]{1,0:T(8,128)S(1)}, u32[]{:S(2)}, u32[]{:S(2)}) collective-permute-start(f32[16,512]{1,0:T(8,128)S(1)} %get-tuple-element.24.refs_0_.refs_3_), channel_id=1, source_target_pairs={{0,1},{1,0},{2,3},{3,2},{4,5},{5,4},{6,7},{7,6},{8,9},{9,8},{10,11... | collective-permute-start | bytes 98312 | tf_op jit(solution)/shard_map/ppermute | solution.py:28
  26.9 1.5 %collective-permute-done.11.refs_2_.refs_5_ = f32[16,512]{1,0:T(8,128)S(1)} collective-permute-done((f32[16,512]{1,0:T(8,128)S(1)}, f32[16,512]{1,0:T(8,128)S(1)}, u32[]{:S(2)}, u32[]{:S(2)}) %collective-permute-start.11) | collective-permute-done | bytes 32800 | tf_op jit(solution)/shard_map/ppermute | solution.py:28
  28.4 2.4 %collective-permute-done.12.refs_3_.refs_6_ = f32[16,512]{1,0:T(8,128)S(1)} collective-permute-done((f32[16,512]{1,0:T(8,128)S(1)}, f32[16,512]{1,0:T(8,128)S(1)}, u32[]{:S(2)}, u32[]{:S(2)}) %collective-permute-start.12) | collective-permute-done | bytes 32800 | tf_op jit(solution)/shard_map/ppermute | solution.py:28
  30.9 4.2 %shard_map.87 = (f32[128,512]{1,0:T(8,128)S(1)}, bf16[128,512]{1,0:T(8,128)(2,1)S(1)}, bf16[128,512]{1,0:T(8,128)(2,1)S(1)}, bf16[128,512]{1,0:T(8,128)(2,1)S(1)...) custom-call(bf16[1024,2048]{1,0:T(8,128)(2,1)S(1)} %get-tuple-element.29.refs_0_, ...), custom_call_target="tpu_custom_call" | custom-call | flops 2147483648 | bytes 7340032 | tf_op jit(solution)/shard_map/pallas_call | solution.py:229
  36.3 2.4 %collective-permute-start.15 = (bf16[128,512]{1,0:T(8,128)(2,1)S(1)}, bf16[128,512]{1,0:T(8,128)(2,1)S(1)}, u32[]{:S(2)}, u32[]{:S(2)}) collective-permute-start(bf16[128,512]{1,0:T(8,128)(2,1)S(1)} %get-tuple-element.28), channel_id=1, source_target_pairs={{0,17},{1,16},{2,19},{3,18},{4,21},{5,20},{6,23},{7,22},{8,25},{9,... | collective-permute-start | bytes 393224 | tf_op jit(solution)/shard_map/ppermute | solution.py:28
  39.2 2.4 %collective-permute-done.13.refs_5_ = bf16[128,512]{1,0:T(8,128)(2,1)S(1)} collective-permute-done((bf16[128,512]{1,0:T(8,128)(2,1)S(1)}, bf16[128,512]{1,0:T(8,128)(2,1)S(1)}, u32[]{:S(2)}, u32[]{:S(2)}) %collective-permute-start.13) | collective-permute-done | bytes 131104 | tf_op jit(solution)/shard_map/ppermute | solution.py:28
  42.1 5.0 %collective-permute-done.14.refs_6_ = bf16[128,512]{1,0:T(8,128)(2,1)S(1)} collective-permute-done((bf16[128,512]{1,0:T(8,128)(2,1)S(1)}, bf16[128,512]{1,0:T(8,128)(2,1)S(1)}, u32[]{:S(2)}, u32[]{:S(2)}) %collective-permute-start.14) | collective-permute-done | bytes 131104 | tf_op jit(solution)/shard_map/ppermute | solution.py:28
  47.1 2.1 %collective-permute-start.16 = (bf16[128,512]{1,0:T(8,128)(2,1)S(1)}, bf16[128,512]{1,0:T(8,128)(2,1)S(1)}, u32[]{:S(2)}, u32[]{:S(2)}) collective-permute-start(bf16[128,512]{1,0:T(8,128)(2,1)S(1)} %get-tuple-element.33), channel_id=1, source_target_pairs={{0,16},{1,17},{2,18},{3,19},{4,20},{5,21},{6,22},{7,23},{8,24},{9,... | collective-permute-start | bytes 393224 | tf_op jit(solution)/shard_map/ppermute | solution.py:28
  49.3 1.3 %shard_map.86 = f32[128,512]{1,0:T(8,128)} custom-call(f32[16,512]{1,0:T(8,128)S(1)} %get-tuple-element.24.refs_0_.refs_3_, f32[16,512]{1,0:T(8,128)S(1)} %collective-permute-done.10.refs_1_.refs_4_, f32[16,512]{1,0:T(8,128)S(1)} %collective-permute-done.11.refs_2_.refs_5_, f32[16,512]{1,0:T(8,128)S(1)} %collective-permute-done.12.refs_3_.refs_6_, ...), custom_call_target="tpu_custom_call" | custom-call | bytes 1048576 | tf_op jit(solution)/shard_map/pallas_call | solution.py:229
  50.7 0.8 %collective-permute-start.22 = (bf16[128,256]{1,0:T(8,128)(2,1)S(1)}, bf16[128,256]{1,0:T(8,128)(2,1)S(1)}, u32[]{:S(2)}, u32[]{:S(2)}) collective-permute-start(bf16[128,256]{1,0:T(8,128)(2,1)S(1)} %get-tuple-element.41), channel_id=1, source_target_pairs={{0,6},{1,7},{2,4},{3,5},{4,2},{5,3},{6,0},{7,1},{8,14},{9,15},{10,... | collective-permute-start | bytes 196616 | tf_op jit(solution)/shard_map/ppermute | solution.py:28
  51.7 3.4 %collective-permute-start.20 = (bf16[128,256]{1,0:T(8,128)(2,1)S(1)}, bf16[128,256]{1,0:T(8,128)(2,1)S(1)}, u32[]{:S(2)}, u32[]{:S(2)}) collective-permute-start(bf16[128,256]{1,0:T(8,128)(2,1)S(1)} %get-tuple-element.40), channel_id=1, source_target_pairs={{0,2},{1,3},{2,0},{3,1},{4,6},{5,7},{6,4},{7,5},{8,10},{9,11},{10,... | collective-permute-start | bytes 196616 | tf_op jit(solution)/shard_map/ppermute | solution.py:28
  55.1 0.8 %add_add_fusion = f32[128,512]{1,0:T(8,128)} fusion(f32[128,512]{1,0:T(8,128)S(1)} %get-tuple-element.32, bf16[128,512]{1,0:T(8,128)(2,1)S(1)} %collective-permute-done.18, bf16[128,512]{1,0:T(8,128)(2,1)S(1)} %collective-permute-done.17, bf16[128,512]{1,0:T(8,128)(2,1)S(1)} %collective-permute-done.16), kind=kLoop, calls=%fused_computation.1 | loop fusion | flops 393216 | bytes 917504 | tf_op jit(solution)/shard_map/add | solution.py:329
  55.9 1.0 %collective-permute-done.22 = bf16[128,256]{1,0:T(8,128)(2,1)S(1)} collective-permute-done((bf16[128,256]{1,0:T(8,128)(2,1)S(1)}, bf16[128,256]{1,0:T(8,128)(2,1)S(1)}, u32[]{:S(2)}, u32[]{:S(2)}) %collective-permute-start.22) | collective-permute-done | bytes 65568 | tf_op jit(solution)/shard_map/ppermute | solution.py:28
  56.9 1.1 %collective-permute-done.21 = bf16[128,256]{1,0:T(8,128)(2,1)S(1)} collective-permute-done((bf16[128,256]{1,0:T(8,128)(2,1)S(1)}, bf16[128,256]{1,0:T(8,128)(2,1)S(1)}, u32[]{:S(2)}, u32[]{:S(2)}) %collective-permute-start.21) | collective-permute-done | bytes 65568 | tf_op jit(solution)/shard_map/ppermute | solution.py:28
  (31 shorter events, 6.2 us)
Async XLA Ops:
  1.7 9.2 %collective-permute-start.3 = (bf16[128,256]{1,0:T(8,128)(2,1)S(1)}, bf16[128,256]{1,0:T(8,128)(2,1)S(1)}, u32[]{:S(2)}, u32[]{:S(2)}) collective-permute-start(bf16[128,256]{1,0:T(8,128)(2,1)S(1)} %get-tuple-element.23.refs_5_.refs_7_), channel_id=1, source_target_pairs={{0,2},{1,3},{2,0},{3,1},{4,6},{5,7},{6,4},{7,5},{8,10},{9,11},{10,... | collective-permute-start | bytes 196616 | tf_op jit(solution)/shard_map/ppermute | solution.py:28
  4.8 14.7 %collective-permute-start = (bf16[128,1024]{1,0:T(8,128)(2,1)S(1)}, bf16[128,1024]{1,0:T(8,128)(2,1)S(1)}, u32[]{:S(2)}, u32[]{:S(2)}) collective-permute-start(bf16[128,1024]{1,0:T(8,128)(2,1)S(1)} %get-tuple-element.22.refs_1_), channel_id=1, source_target_pairs={{0,16},{1,17},{2,18},{3,19},{4,20},{5,21},{6,22},{7,23},{8,24},{9,... | collective-permute-start | bytes 786440 | tf_op jit(solution)/shard_map/ppermute | solution.py:28
  6.3 13.2 %collective-permute-start.1 = (bf16[128,1024]{1,0:T(8,128)(2,1)S(1)}, bf16[128,1024]{1,0:T(8,128)(2,1)S(1)}, u32[]{:S(2)}, u32[]{:S(2)}) collective-permute-start(bf16[128,1024]{1,0:T(8,128)(2,1)S(1)} %get-tuple-element.22.refs_1_), channel_id=1, source_target_pairs={{0,1},{1,0},{2,3},{3,2},{4,5},{5,4},{6,7},{7,6},{8,9},{9,8},{10,11... | collective-permute-start | bytes 786440 | tf_op jit(solution)/shard_map/ppermute | solution.py:28
  7.8 11.7 %collective-permute-start.2 = (bf16[128,1024]{1,0:T(8,128)(2,1)S(1)}, bf16[128,1024]{1,0:T(8,128)(2,1)S(1)}, u32[]{:S(2)}, u32[]{:S(2)}) collective-permute-start(bf16[128,1024]{1,0:T(8,128)(2,1)S(1)} %get-tuple-element.22.refs_1_), channel_id=1, source_target_pairs={{0,17},{1,16},{2,19},{3,18},{4,21},{5,20},{6,23},{7,22},{8,25},{9,... | collective-permute-start | bytes 786440 | tf_op jit(solution)/shard_map/ppermute | solution.py:28
  8.3 6.3 %collective-permute-start.4 = (bf16[128,256]{1,0:T(8,128)(2,1)S(1)}, bf16[128,256]{1,0:T(8,128)(2,1)S(1)}, u32[]{:S(2)}, u32[]{:S(2)}) collective-permute-start(bf16[128,256]{1,0:T(8,128)(2,1)S(1)} %get-tuple-element.23.refs_5_.refs_7_), channel_id=1, source_target_pairs={{0,4},{1,5},{2,6},{3,7},{4,0},{5,1},{6,2},{7,3},{8,12},{9,13},{10,... | collective-permute-start | bytes 196616 | tf_op jit(solution)/shard_map/ppermute | solution.py:28
  10.9 6.1 %collective-permute-start.5 = (bf16[128,256]{1,0:T(8,128)(2,1)S(1)}, bf16[128,256]{1,0:T(8,128)(2,1)S(1)}, u32[]{:S(2)}, u32[]{:S(2)}) collective-permute-start(bf16[128,256]{1,0:T(8,128)(2,1)S(1)} %get-tuple-element.23.refs_5_.refs_7_), channel_id=1, source_target_pairs={{0,6},{1,7},{2,4},{3,5},{4,2},{5,3},{6,0},{7,1},{8,14},{9,15},{10,... | collective-permute-start | bytes 196616 | tf_op jit(solution)/shard_map/ppermute | solution.py:28
  14.6 2.3 %collective-permute-start.6 = (bf16[128,256]{1,0:T(8,128)(2,1)S(1)}, bf16[128,256]{1,0:T(8,128)(2,1)S(1)}, u32[]{:S(2)}, u32[]{:S(2)}) collective-permute-start(bf16[128,256]{1,0:T(8,128)(2,1)S(1)} %get-tuple-element.23.refs_5_.refs_7_), channel_id=1, source_target_pairs={{0,8},{1,9},{2,10},{3,11},{4,12},{5,13},{6,14},{7,15},{8,0},{9,1},... | collective-permute-start | bytes 196616 | tf_op jit(solution)/shard_map/ppermute | solution.py:28
  16.9 1.3 %collective-permute-start.7 = (bf16[128,256]{1,0:T(8,128)(2,1)S(1)}, bf16[128,256]{1,0:T(8,128)(2,1)S(1)}, u32[]{:S(2)}, u32[]{:S(2)}) collective-permute-start(bf16[128,256]{1,0:T(8,128)(2,1)S(1)} %collective-permute-done.3.refs_6_.refs_8_), channel_id=1, source_target_pairs={{0,8},{1,9},{2,10},{3,11},{4,12},{5,13},{6,14},{7,15},{8,0},{9,1},... | collective-permute-start | bytes 196616 | tf_op jit(solution)/shard_map/ppermute | solution.py:28
  16.9 1.4 %collective-permute-start.8 = (bf16[128,256]{1,0:T(8,128)(2,1)S(1)}, bf16[128,256]{1,0:T(8,128)(2,1)S(1)}, u32[]{:S(2)}, u32[]{:S(2)}) collective-permute-start(bf16[128,256]{1,0:T(8,128)(2,1)S(1)} %collective-permute-done.4.refs_7_.refs_9_), channel_id=1, source_target_pairs={{0,8},{1,9},{2,10},{3,11},{4,12},{5,13},{6,14},{7,15},{8,0},{9,1},... | collective-permute-start | bytes 196616 | tf_op jit(solution)/shard_map/ppermute | solution.py:28
  18.2 1.3 %collective-permute-start.9 = (bf16[128,256]{1,0:T(8,128)(2,1)S(1)}, bf16[128,256]{1,0:T(8,128)(2,1)S(1)}, u32[]{:S(2)}, u32[]{:S(2)}) collective-permute-start(bf16[128,256]{1,0:T(8,128)(2,1)S(1)} %collective-permute-done.5.refs_8_.refs_10_), channel_id=1, source_target_pairs={{0,8},{1,9},{2,10},{3,11},{4,12},{5,13},{6,14},{7,15},{8,0},{9,1},... | collective-permute-start | bytes 196616 | tf_op jit(solution)/shard_map/ppermute | solution.py:28
  23.0 4.0 %collective-permute-start.10 = (f32[16,512]{1,0:T(8,128)S(1)}, f32[16,512]{1,0:T(8,128)S(1)}, u32[]{:S(2)}, u32[]{:S(2)}) collective-permute-start(f32[16,512]{1,0:T(8,128)S(1)} %get-tuple-element.24.refs_0_.refs_3_), channel_id=1, source_target_pairs={{0,16},{1,17},{2,18},{3,19},{4,20},{5,21},{6,22},{7,23},{8,24},{9,... | collective-permute-start | bytes 98312 | tf_op jit(solution)/shard_map/ppermute | solution.py:28
  24.5 3.9 %collective-permute-start.11 = (f32[16,512]{1,0:T(8,128)S(1)}, f32[16,512]{1,0:T(8,128)S(1)}, u32[]{:S(2)}, u32[]{:S(2)}) collective-permute-start(f32[16,512]{1,0:T(8,128)S(1)} %get-tuple-element.24.refs_0_.refs_3_), channel_id=1, source_target_pairs={{0,1},{1,0},{2,3},{3,2},{4,5},{5,4},{6,7},{7,6},{8,9},{9,8},{10,11... | collective-permute-start | bytes 98312 | tf_op jit(solution)/shard_map/ppermute | solution.py:28
  26.0 4.8 %collective-permute-start.12 = (f32[16,512]{1,0:T(8,128)S(1)}, f32[16,512]{1,0:T(8,128)S(1)}, u32[]{:S(2)}, u32[]{:S(2)}) collective-permute-start(f32[16,512]{1,0:T(8,128)S(1)} %get-tuple-element.24.refs_0_.refs_3_), channel_id=1, source_target_pairs={{0,17},{1,16},{2,19},{3,18},{4,21},{5,20},{6,23},{7,22},{8,25},{9,... | collective-permute-start | bytes 98312 | tf_op jit(solution)/shard_map/ppermute | solution.py:28
  35.1 15.5 %collective-permute-start.19 = (bf16[512,256]{1,0:T(8,128)(2,1)S(1)}, bf16[512,256]{1,0:T(8,128)(2,1)S(1)}, u32[]{:S(2)}, u32[]{:S(2)}) collective-permute-start(bf16[512,256]{1,0:T(8,128)(2,1)S(1)} %get-tuple-element.37), channel_id=1, source_target_pairs={{0,8},{1,9},{2,10},{3,11},{4,12},{5,13},{6,14},{7,15},{8,0},{9,1},... | collective-permute-start | bytes 786440 | tf_op jit(solution)/shard_map/ppermute | solution.py:28
  35.2 6.4 %collective-permute-start.13 = (bf16[128,512]{1,0:T(8,128)(2,1)S(1)}, bf16[128,512]{1,0:T(8,128)(2,1)S(1)}, u32[]{:S(2)}, u32[]{:S(2)}) collective-permute-start(bf16[128,512]{1,0:T(8,128)(2,1)S(1)} %get-tuple-element.26), channel_id=1, source_target_pairs={{0,16},{1,17},{2,18},{3,19},{4,20},{5,21},{6,22},{7,23},{8,24},{9,... | collective-permute-start | bytes 393224 | tf_op jit(solution)/shard_map/ppermute | solution.py:28
  35.8 11.3 %collective-permute-start.14 = (bf16[128,512]{1,0:T(8,128)(2,1)S(1)}, bf16[128,512]{1,0:T(8,128)(2,1)S(1)}, u32[]{:S(2)}, u32[]{:S(2)}) collective-permute-start(bf16[128,512]{1,0:T(8,128)(2,1)S(1)} %get-tuple-element.27), channel_id=1, source_target_pairs={{0,1},{1,0},{2,3},{3,2},{4,5},{5,4},{6,7},{7,6},{8,9},{9,8},{10,11... | collective-permute-start | bytes 393224 | tf_op jit(solution)/shard_map/ppermute | solution.py:28
  36.3 13.0 %collective-permute-start.15 = (bf16[128,512]{1,0:T(8,128)(2,1)S(1)}, bf16[128,512]{1,0:T(8,128)(2,1)S(1)}, u32[]{:S(2)}, u32[]{:S(2)}) collective-permute-start(bf16[128,512]{1,0:T(8,128)(2,1)S(1)} %get-tuple-element.28), channel_id=1, source_target_pairs={{0,17},{1,16},{2,19},{3,18},{4,21},{5,20},{6,23},{7,22},{8,25},{9,... | collective-permute-start | bytes 393224 | tf_op jit(solution)/shard_map/ppermute | solution.py:28
  38.7 13.0 %collective-permute-start.18 = (bf16[128,512]{1,0:T(8,128)(2,1)S(1)}, bf16[128,512]{1,0:T(8,128)(2,1)S(1)}, u32[]{:S(2)}, u32[]{:S(2)}) collective-permute-start(bf16[128,512]{1,0:T(8,128)(2,1)S(1)} %get-tuple-element.35), channel_id=1, source_target_pairs={{0,17},{1,16},{2,19},{3,18},{4,21},{5,20},{6,23},{7,22},{8,25},{9,... | collective-permute-start | bytes 393224 | tf_op jit(solution)/shard_map/ppermute | solution.py:28
  41.6 13.5 %collective-permute-start.17 = (bf16[128,512]{1,0:T(8,128)(2,1)S(1)}, bf16[128,512]{1,0:T(8,128)(2,1)S(1)}, u32[]{:S(2)}, u32[]{:S(2)}) collective-permute-start(bf16[128,512]{1,0:T(8,128)(2,1)S(1)} %get-tuple-element.34), channel_id=1, source_target_pairs={{0,1},{1,0},{2,3},{3,2},{4,5},{5,4},{6,7},{7,6},{8,9},{9,8},{10,11... | collective-permute-start | bytes 393224 | tf_op jit(solution)/shard_map/ppermute | solution.py:28
  47.1 8.0 %collective-permute-start.16 = (bf16[128,512]{1,0:T(8,128)(2,1)S(1)}, bf16[128,512]{1,0:T(8,128)(2,1)S(1)}, u32[]{:S(2)}, u32[]{:S(2)}) collective-permute-start(bf16[128,512]{1,0:T(8,128)(2,1)S(1)} %get-tuple-element.33), channel_id=1, source_target_pairs={{0,16},{1,17},{2,18},{3,19},{4,20},{5,21},{6,22},{7,23},{8,24},{9,... | collective-permute-start | bytes 393224 | tf_op jit(solution)/shard_map/ppermute | solution.py:28
  50.7 6.3 %collective-permute-start.22 = (bf16[128,256]{1,0:T(8,128)(2,1)S(1)}, bf16[128,256]{1,0:T(8,128)(2,1)S(1)}, u32[]{:S(2)}, u32[]{:S(2)}) collective-permute-start(bf16[128,256]{1,0:T(8,128)(2,1)S(1)} %get-tuple-element.41), channel_id=1, source_target_pairs={{0,6},{1,7},{2,4},{3,5},{4,2},{5,3},{6,0},{7,1},{8,14},{9,15},{10,... | collective-permute-start | bytes 196616 | tf_op jit(solution)/shard_map/ppermute | solution.py:28
  51.5 6.6 %collective-permute-start.21 = (bf16[128,256]{1,0:T(8,128)(2,1)S(1)}, bf16[128,256]{1,0:T(8,128)(2,1)S(1)}, u32[]{:S(2)}, u32[]{:S(2)}) collective-permute-start(bf16[128,256]{1,0:T(8,128)(2,1)S(1)} %get-tuple-element.42), channel_id=1, source_target_pairs={{0,4},{1,5},{2,6},{3,7},{4,0},{5,1},{6,2},{7,3},{8,12},{9,13},{10,... | collective-permute-start | bytes 196616 | tf_op jit(solution)/shard_map/ppermute | solution.py:28
  51.7 6.3 %collective-permute-start.20 = (bf16[128,256]{1,0:T(8,128)(2,1)S(1)}, bf16[128,256]{1,0:T(8,128)(2,1)S(1)}, u32[]{:S(2)}, u32[]{:S(2)}) collective-permute-start(bf16[128,256]{1,0:T(8,128)(2,1)S(1)} %get-tuple-element.40), channel_id=1, source_target_pairs={{0,2},{1,3},{2,0},{3,1},{4,6},{5,7},{6,4},{7,5},{8,10},{9,11},{10,... | collective-permute-start | bytes 196616 | tf_op jit(solution)/shard_map/ppermute | solution.py:28

commit v4 on v3

--- a/solution.py
+++ b/solution.py
@@ -97,7 +97,8 @@
         span = slice(j * tok, (j + 1) * tok)
         kk_ref[span, :dim] = ref[:, :dim]
         kk_ref[span, dim:] = ref[:, :dim]
-        v_ref[span, :] = ref[:, dim:]
+        v_ref[span, :dim] = ref[:, dim:]
+        v_ref[span, dim:] = jnp.ones((tok, dim), BF16)
 
     def score(r):
         q = by_head(qds[r], dim, 0, width)
@@ -122,16 +123,14 @@
         top = jnp.maximum(top, FLOOR)
         if r + 1 < nr:
             score(r + 1)
-        total = None
         for j in range(nk):
             span = slice(j * tok, (j + 1) * tok)
             p = jnp.exp2(s_ref[slot, span, :] - (top + biases[j]))
-            part = jnp.sum(p, axis=0, keepdims=True)
-            total = part if total is None else total + part
             p_ref[span, lanes] = p.astype(BF16)
         d = by_head(qds[r], dim, width, width)
         dt_ref[:, lanes] = d
-        out = tn(v_ref[...], p_ref[:, lanes])
+        out = tn(v_ref[:, : dim + 16], p_ref[:, lanes])
+        out, total = out[:dim], out[dim : dim + 1]
         for h in range(width // dim):
             piece = out[:, h * tok : (h + 1) * tok].astype(outs[r].dtype).T
             outs[r][:, h * dim : (h + 1) * dim] = piece
@@ -294,7 +293,7 @@
         ]
         + [shape((tok, width), BF16)] * (nr - 1),
         bias, *qd, *kv,
-        scratch=[wide, narrow, score], flops=2 * work, room=room + (6 << 20),
+        scratch=[wide, wide, score], flops=2 * work, room=room + (6 << 20),
     )
     all_stats = [stats] + spray([stats] * (nr - 1), row_masks)
     all_parts = parts[:1] + spray(parts[1:], row_masks)

time: 58.9 us -> 58.2 us (0.988)
  Pallas kernels: 10.1 us -> 9.35 us
    pallas_call x4, Pallas kernels: 10.1 us -> 9.35 us  [call(): pl.pallas_call(kernel, out_shape=outs, in_specs=[SMEM] * scalars + [space...]
where the time goes in v4:
time: 58.2 us; the launch traced here: 58.1 us
  starting transfers between devices  24.9 us (43%)
  waiting for transfers between devices  21.6 us (37%)
  Pallas kernels  9.35 us (16%)
  other arithmetic  0.87 us (1%)
  between operations  0.71 us (1%)
  local copies, waits for them, and re-layouts  0.67 us (1%)
    ppermute x23, starting transfers between devices, swap(): return lax.ppermute(value, AXES, [(i, i ^ mask) for i in range(devices)])  24.9 us
    ppermute x23, waiting for transfers between devices, swap(): return lax.ppermute(value, AXES, [(i, i ^ mask) for i in range(devices)])  21.6 us
    pallas_call x4, Pallas kernels, call(): pl.pallas_call(kernel, out_shape=outs, in_specs=[SMEM] * scalars + [space...  9.35 us
  transfers between devices with their start and end apart: 23, of which 11 were waited for; matrix products, arithmetic and copies ran while one was open for 1% of the time, Pallas kernels for 2%

profile of v4, /device:TPU:0, one launch (start us, length us, event | category | flops | bytes accessed | tf_op | source)
XLA Modules:
  0.0 58.1 jit_solution(9688693868611308808)
XLA Ops:
  0.6 1.0 %shard_map.84 = (bf16[128,1024]{1,0:T(8,128)(2,1)S(1)}, bf16[128,256]{1,0:T(8,128)(2,1)S(1)}, f32[4,128]{1,0:T(4,128)S(1)}) custom-call(s32[1]{0:T(128)} %bitcast.refs_0_, s32[32]{0:T(128)} %refs_1_.1, bf16[128,512]{1,0:T(8,128)(2,1)} %refs_2_.1, bf16[128,512]{1,0:T(8,128)(2,1)} %refs_3_.1, bf16[128,128]{1,0:T(8,128)(2,1)} %refs_4_.1, bf16[128,128]{1,0:T(8,128)(2,1)} %refs_5_.1), custom_call_target="tpu_custom_call" | custom-call | bytes 657540 | tf_op jit(solution)/shard_map/pallas_call | solution.py:228
  1.7 3.1 %collective-permute-start.3 = (bf16[128,256]{1,0:T(8,128)(2,1)S(1)}, bf16[128,256]{1,0:T(8,128)(2,1)S(1)}, u32[]{:S(2)}, u32[]{:S(2)}) collective-permute-start(bf16[128,256]{1,0:T(8,128)(2,1)S(1)} %get-tuple-element.23.refs_5_.refs_7_), channel_id=1, source_target_pairs={{0,2},{1,3},{2,0},{3,1},{4,6},{5,7},{6,4},{7,5},{8,10},{9,11},{10,... | collective-permute-start | bytes 196616 | tf_op jit(solution)/shard_map/ppermute | solution.py:28
  4.8 1.5 %collective-permute-start = (bf16[128,1024]{1,0:T(8,128)(2,1)S(1)}, bf16[128,1024]{1,0:T(8,128)(2,1)S(1)}, u32[]{:S(2)}, u32[]{:S(2)}) collective-permute-start(bf16[128,1024]{1,0:T(8,128)(2,1)S(1)} %get-tuple-element.22.refs_1_), channel_id=1, source_target_pairs={{0,16},{1,17},{2,18},{3,19},{4,20},{5,21},{6,22},{7,23},{8,24},{9,... | collective-permute-start | bytes 786440 | tf_op jit(solution)/shard_map/ppermute | solution.py:28
  6.3 1.5 %collective-permute-start.1 = (bf16[128,1024]{1,0:T(8,128)(2,1)S(1)}, bf16[128,1024]{1,0:T(8,128)(2,1)S(1)}, u32[]{:S(2)}, u32[]{:S(2)}) collective-permute-start(bf16[128,1024]{1,0:T(8,128)(2,1)S(1)} %get-tuple-element.22.refs_1_), channel_id=1, source_target_pairs={{0,1},{1,0},{2,3},{3,2},{4,5},{5,4},{6,7},{7,6},{8,9},{9,8},{10,11... | collective-permute-start | bytes 786440 | tf_op jit(solution)/shard_map/ppermute | solution.py:28
  8.3 2.6 %collective-permute-start.4 = (bf16[128,256]{1,0:T(8,128)(2,1)S(1)}, bf16[128,256]{1,0:T(8,128)(2,1)S(1)}, u32[]{:S(2)}, u32[]{:S(2)}) collective-permute-start(bf16[128,256]{1,0:T(8,128)(2,1)S(1)} %get-tuple-element.23.refs_5_.refs_7_), channel_id=1, source_target_pairs={{0,4},{1,5},{2,6},{3,7},{4,0},{5,1},{6,2},{7,3},{8,12},{9,13},{10,... | collective-permute-start | bytes 196616 | tf_op jit(solution)/shard_map/ppermute | solution.py:28
  11.1 3.5 %collective-permute-done.4.refs_7_.refs_9_ = bf16[128,256]{1,0:T(8,128)(2,1)S(1)} collective-permute-done((bf16[128,256]{1,0:T(8,128)(2,1)S(1)}, bf16[128,256]{1,0:T(8,128)(2,1)S(1)}, u32[]{:S(2)}, u32[]{:S(2)}) %collective-permute-start.4) | collective-permute-done | bytes 65568 | tf_op jit(solution)/shard_map/ppermute | solution.py:28
  14.6 2.3 %collective-permute-done.5.refs_8_.refs_10_ = bf16[128,256]{1,0:T(8,128)(2,1)S(1)} collective-permute-done((bf16[128,256]{1,0:T(8,128)(2,1)S(1)}, bf16[128,256]{1,0:T(8,128)(2,1)S(1)}, u32[]{:S(2)}, u32[]{:S(2)}) %collective-permute-start.5) | collective-permute-done | bytes 65568 | tf_op jit(solution)/shard_map/ppermute | solution.py:28
  18.3 1.1 %collective-permute-done.9.refs_12_.refs_14_ = bf16[128,256]{1,0:T(8,128)(2,1)S(1)} collective-permute-done((bf16[128,256]{1,0:T(8,128)(2,1)S(1)}, bf16[128,256]{1,0:T(8,128)(2,1)S(1)}, u32[]{:S(2)}, u32[]{:S(2)}) %collective-permute-start.9) | collective-permute-done | bytes 65568 | tf_op jit(solution)/shard_map/ppermute | solution.py:28
  19.5 2.8 %shard_map.85 = (f32[16,512]{1,0:T(8,128)S(1)}, bf16[1024,2048]{1,0:T(8,128)(2,1)S(1)}, bf16[128,2048]{1,0:T(8,128)(2,1)S(1)}, bf16[128,2048]{1,0:T(8,128)(2,1)S...) custom-call(f32[4,128]{1,0:T(4,128)S(1)} %get-tuple-element.21.refs_, ...), custom_call_target="tpu_custom_call" | custom-call | flops 1073741824 | bytes 7505920 | tf_op jit(solution)/shard_map/pallas_call | solution.py:228
  22.3 1.6 %collective-permute-start.10 = (f32[16,512]{1,0:T(8,128)S(1)}, f32[16,512]{1,0:T(8,128)S(1)}, u32[]{:S(2)}, u32[]{:S(2)}) collective-permute-start(f32[16,512]{1,0:T(8,128)S(1)} %get-tuple-element.24.refs_0_.refs_3_), channel_id=1, source_target_pairs={{0,16},{1,17},{2,18},{3,19},{4,20},{5,21},{6,22},{7,23},{8,24},{9,... | collective-permute-start | bytes 98312 | tf_op jit(solution)/shard_map/ppermute | solution.py:28
  23.8 1.5 %collective-permute-start.11 = (f32[16,512]{1,0:T(8,128)S(1)}, f32[16,512]{1,0:T(8,128)S(1)}, u32[]{:S(2)}, u32[]{:S(2)}) collective-permute-start(f32[16,512]{1,0:T(8,128)S(1)} %get-tuple-element.24.refs_0_.refs_3_), channel_id=1, source_target_pairs={{0,1},{1,0},{2,3},{3,2},{4,5},{5,4},{6,7},{7,6},{8,9},{9,8},{10,11... | collective-permute-start | bytes 98312 | tf_op jit(solution)/shard_map/ppermute | solution.py:28
  26.2 1.5 %collective-permute-done.11.refs_2_.refs_5_ = f32[16,512]{1,0:T(8,128)S(1)} collective-permute-done((f32[16,512]{1,0:T(8,128)S(1)}, f32[16,512]{1,0:T(8,128)S(1)}, u32[]{:S(2)}, u32[]{:S(2)}) %collective-permute-start.11) | collective-permute-done | bytes 32800 | tf_op jit(solution)/shard_map/ppermute | solution.py:28
  27.7 2.4 %collective-permute-done.12.refs_3_.refs_6_ = f32[16,512]{1,0:T(8,128)S(1)} collective-permute-done((f32[16,512]{1,0:T(8,128)S(1)}, f32[16,512]{1,0:T(8,128)S(1)}, u32[]{:S(2)}, u32[]{:S(2)}) %collective-permute-start.12) | collective-permute-done | bytes 32800 | tf_op jit(solution)/shard_map/ppermute | solution.py:28
  30.2 4.2 %shard_map.87 = (f32[128,512]{1,0:T(8,128)S(1)}, bf16[128,512]{1,0:T(8,128)(2,1)S(1)}, bf16[128,512]{1,0:T(8,128)(2,1)S(1)}, bf16[128,512]{1,0:T(8,128)(2,1)S(1)...) custom-call(bf16[1024,2048]{1,0:T(8,128)(2,1)S(1)} %get-tuple-element.29.refs_0_, ...), custom_call_target="tpu_custom_call" | custom-call | flops 2147483648 | bytes 7340032 | tf_op jit(solution)/shard_map/pallas_call | solution.py:228
  35.6 2.5 %collective-permute-start.15 = (bf16[128,512]{1,0:T(8,128)(2,1)S(1)}, bf16[128,512]{1,0:T(8,128)(2,1)S(1)}, u32[]{:S(2)}, u32[]{:S(2)}) collective-permute-start(bf16[128,512]{1,0:T(8,128)(2,1)S(1)} %get-tuple-element.28), channel_id=1, source_target_pairs={{0,17},{1,16},{2,19},{3,18},{4,21},{5,20},{6,23},{7,22},{8,25},{9,... | collective-permute-start | bytes 393224 | tf_op jit(solution)/shard_map/ppermute | solution.py:28
  38.5 2.4 %collective-permute-done.13.refs_5_ = bf16[128,512]{1,0:T(8,128)(2,1)S(1)} collective-permute-done((bf16[128,512]{1,0:T(8,128)(2,1)S(1)}, bf16[128,512]{1,0:T(8,128)(2,1)S(1)}, u32[]{:S(2)}, u32[]{:S(2)}) %collective-permute-start.13) | collective-permute-done | bytes 131104 | tf_op jit(solution)/shard_map/ppermute | solution.py:28
  41.4 4.9 %collective-permute-done.14.refs_6_ = bf16[128,512]{1,0:T(8,128)(2,1)S(1)} collective-permute-done((bf16[128,512]{1,0:T(8,128)(2,1)S(1)}, bf16[128,512]{1,0:T(8,128)(2,1)S(1)}, u32[]{:S(2)}, u32[]{:S(2)}) %collective-permute-start.14) | collective-permute-done | bytes 131104 | tf_op jit(solution)/shard_map/ppermute | solution.py:28
  46.4 2.2 %collective-permute-start.16 = (bf16[128,512]{1,0:T(8,128)(2,1)S(1)}, bf16[128,512]{1,0:T(8,128)(2,1)S(1)}, u32[]{:S(2)}, u32[]{:S(2)}) collective-permute-start(bf16[128,512]{1,0:T(8,128)(2,1)S(1)} %get-tuple-element.33), channel_id=1, source_target_pairs={{0,16},{1,17},{2,18},{3,19},{4,20},{5,21},{6,22},{7,23},{8,24},{9,... | collective-permute-start | bytes 393224 | tf_op jit(solution)/shard_map/ppermute | solution.py:28
  48.6 1.3 %shard_map.86 = f32[128,512]{1,0:T(8,128)} custom-call(f32[16,512]{1,0:T(8,128)S(1)} %get-tuple-element.24.refs_0_.refs_3_, f32[16,512]{1,0:T(8,128)S(1)} %collective-permute-done.10.refs_1_.refs_4_, f32[16,512]{1,0:T(8,128)S(1)} %collective-permute-done.11.refs_2_.refs_5_, f32[16,512]{1,0:T(8,128)S(1)} %collective-permute-done.12.refs_3_.refs_6_, ...), custom_call_target="tpu_custom_call" | custom-call | bytes 1048576 | tf_op jit(solution)/shard_map/pallas_call | solution.py:228
  50.0 0.8 %collective-permute-start.22 = (bf16[128,256]{1,0:T(8,128)(2,1)S(1)}, bf16[128,256]{1,0:T(8,128)(2,1)S(1)}, u32[]{:S(2)}, u32[]{:S(2)}) collective-permute-start(bf16[128,256]{1,0:T(8,128)(2,1)S(1)} %get-tuple-element.41), channel_id=1, source_target_pairs={{0,6},{1,7},{2,4},{3,5},{4,2},{5,3},{6,0},{7,1},{8,14},{9,15},{10,... | collective-permute-start | bytes 196616 | tf_op jit(solution)/shard_map/ppermute | solution.py:28
  51.0 3.4 %collective-permute-start.20 = (bf16[128,256]{1,0:T(8,128)(2,1)S(1)}, bf16[128,256]{1,0:T(8,128)(2,1)S(1)}, u32[]{:S(2)}, u32[]{:S(2)}) collective-permute-start(bf16[128,256]{1,0:T(8,128)(2,1)S(1)} %get-tuple-element.40), channel_id=1, source_target_pairs={{0,2},{1,3},{2,0},{3,1},{4,6},{5,7},{6,4},{7,5},{8,10},{9,11},{10,... | collective-permute-start | bytes 196616 | tf_op jit(solution)/shard_map/ppermute | solution.py:28
  54.4 0.8 %add_add_fusion = f32[128,512]{1,0:T(8,128)} fusion(f32[128,512]{1,0:T(8,128)S(1)} %get-tuple-element.32, bf16[128,512]{1,0:T(8,128)(2,1)S(1)} %collective-permute-done.18, bf16[128,512]{1,0:T(8,128)(2,1)S(1)} %collective-permute-done.17, bf16[128,512]{1,0:T(8,128)(2,1)S(1)} %collective-permute-done.16), kind=kLoop, calls=%fused_computation.1 | loop fusion | flops 393216 | bytes 917504 | tf_op jit(solution)/shard_map/add | solution.py:328
  55.2 1.0 %collective-permute-done.22 = bf16[128,256]{1,0:T(8,128)(2,1)S(1)} collective-permute-done((bf16[128,256]{1,0:T(8,128)(2,1)S(1)}, bf16[128,256]{1,0:T(8,128)(2,1)S(1)}, u32[]{:S(2)}, u32[]{:S(2)}) %collective-permute-start.22) | collective-permute-done | bytes 65568 | tf_op jit(solution)/shard_map/ppermute | solution.py:28
  56.2 1.2 %collective-permute-done.21 = bf16[128,256]{1,0:T(8,128)(2,1)S(1)} collective-permute-done((bf16[128,256]{1,0:T(8,128)(2,1)S(1)}, bf16[128,256]{1,0:T(8,128)(2,1)S(1)}, u32[]{:S(2)}, u32[]{:S(2)}) %collective-permute-start.21) | collective-permute-done | bytes 65568 | tf_op jit(solution)/shard_map/ppermute | solution.py:28
  (31 shorter events, 6.1 us)
Async XLA Ops:
  1.7 9.2 %collective-permute-start.3 = (bf16[128,256]{1,0:T(8,128)(2,1)S(1)}, bf16[128,256]{1,0:T(8,128)(2,1)S(1)}, u32[]{:S(2)}, u32[]{:S(2)}) collective-permute-start(bf16[128,256]{1,0:T(8,128)(2,1)S(1)} %get-tuple-element.23.refs_5_.refs_7_), channel_id=1, source_target_pairs={{0,2},{1,3},{2,0},{3,1},{4,6},{5,7},{6,4},{7,5},{8,10},{9,11},{10,... | collective-permute-start | bytes 196616 | tf_op jit(solution)/shard_map/ppermute | solution.py:28
  4.8 14.7 %collective-permute-start = (bf16[128,1024]{1,0:T(8,128)(2,1)S(1)}, bf16[128,1024]{1,0:T(8,128)(2,1)S(1)}, u32[]{:S(2)}, u32[]{:S(2)}) collective-permute-start(bf16[128,1024]{1,0:T(8,128)(2,1)S(1)} %get-tuple-element.22.refs_1_), channel_id=1, source_target_pairs={{0,16},{1,17},{2,18},{3,19},{4,20},{5,21},{6,22},{7,23},{8,24},{9,... | collective-permute-start | bytes 786440 | tf_op jit(solution)/shard_map/ppermute | solution.py:28
  6.3 13.2 %collective-permute-start.1 = (bf16[128,1024]{1,0:T(8,128)(2,1)S(1)}, bf16[128,1024]{1,0:T(8,128)(2,1)S(1)}, u32[]{:S(2)}, u32[]{:S(2)}) collective-permute-start(bf16[128,1024]{1,0:T(8,128)(2,1)S(1)} %get-tuple-element.22.refs_1_), channel_id=1, source_target_pairs={{0,1},{1,0},{2,3},{3,2},{4,5},{5,4},{6,7},{7,6},{8,9},{9,8},{10,11... | collective-permute-start | bytes 786440 | tf_op jit(solution)/shard_map/ppermute | solution.py:28
  7.8 11.7 %collective-permute-start.2 = (bf16[128,1024]{1,0:T(8,128)(2,1)S(1)}, bf16[128,1024]{1,0:T(8,128)(2,1)S(1)}, u32[]{:S(2)}, u32[]{:S(2)}) collective-permute-start(bf16[128,1024]{1,0:T(8,128)(2,1)S(1)} %get-tuple-element.22.refs_1_), channel_id=1, source_target_pairs={{0,17},{1,16},{2,19},{3,18},{4,21},{5,20},{6,23},{7,22},{8,25},{9,... | collective-permute-start | bytes 786440 | tf_op jit(solution)/shard_map/ppermute | solution.py:28
  8.3 6.3 %collective-permute-start.4 = (bf16[128,256]{1,0:T(8,128)(2,1)S(1)}, bf16[128,256]{1,0:T(8,128)(2,1)S(1)}, u32[]{:S(2)}, u32[]{:S(2)}) collective-permute-start(bf16[128,256]{1,0:T(8,128)(2,1)S(1)} %get-tuple-element.23.refs_5_.refs_7_), channel_id=1, source_target_pairs={{0,4},{1,5},{2,6},{3,7},{4,0},{5,1},{6,2},{7,3},{8,12},{9,13},{10,... | collective-permute-start | bytes 196616 | tf_op jit(solution)/shard_map/ppermute | solution.py:28
  10.9 6.1 %collective-permute-start.5 = (bf16[128,256]{1,0:T(8,128)(2,1)S(1)}, bf16[128,256]{1,0:T(8,128)(2,1)S(1)}, u32[]{:S(2)}, u32[]{:S(2)}) collective-permute-start(bf16[128,256]{1,0:T(8,128)(2,1)S(1)} %get-tuple-element.23.refs_5_.refs_7_), channel_id=1, source_target_pairs={{0,6},{1,7},{2,4},{3,5},{4,2},{5,3},{6,0},{7,1},{8,14},{9,15},{10,... | collective-permute-start | bytes 196616 | tf_op jit(solution)/shard_map/ppermute | solution.py:28
  14.6 2.3 %collective-permute-start.6 = (bf16[128,256]{1,0:T(8,128)(2,1)S(1)}, bf16[128,256]{1,0:T(8,128)(2,1)S(1)}, u32[]{:S(2)}, u32[]{:S(2)}) collective-permute-start(bf16[128,256]{1,0:T(8,128)(2,1)S(1)} %get-tuple-element.23.refs_5_.refs_7_), channel_id=1, source_target_pairs={{0,8},{1,9},{2,10},{3,11},{4,12},{5,13},{6,14},{7,15},{8,0},{9,1},... | collective-permute-start | bytes 196616 | tf_op jit(solution)/shard_map/ppermute | solution.py:28
  16.9 1.3 %collective-permute-start.7 = (bf16[128,256]{1,0:T(8,128)(2,1)S(1)}, bf16[128,256]{1,0:T(8,128)(2,1)S(1)}, u32[]{:S(2)}, u32[]{:S(2)}) collective-permute-start(bf16[128,256]{1,0:T(8,128)(2,1)S(1)} %collective-permute-done.3.refs_6_.refs_8_), channel_id=1, source_target_pairs={{0,8},{1,9},{2,10},{3,11},{4,12},{5,13},{6,14},{7,15},{8,0},{9,1},... | collective-permute-start | bytes 196616 | tf_op jit(solution)/shard_map/ppermute | solution.py:28
  16.9 1.4 %collective-permute-start.8 = (bf16[128,256]{1,0:T(8,128)(2,1)S(1)}, bf16[128,256]{1,0:T(8,128)(2,1)S(1)}, u32[]{:S(2)}, u32[]{:S(2)}) collective-permute-start(bf16[128,256]{1,0:T(8,128)(2,1)S(1)} %collective-permute-done.4.refs_7_.refs_9_), channel_id=1, source_target_pairs={{0,8},{1,9},{2,10},{3,11},{4,12},{5,13},{6,14},{7,15},{8,0},{9,1},... | collective-permute-start | bytes 196616 | tf_op jit(solution)/shard_map/ppermute | solution.py:28
  18.2 1.3 %collective-permute-start.9 = (bf16[128,256]{1,0:T(8,128)(2,1)S(1)}, bf16[128,256]{1,0:T(8,128)(2,1)S(1)}, u32[]{:S(2)}, u32[]{:S(2)}) collective-permute-start(bf16[128,256]{1,0:T(8,128)(2,1)S(1)} %collective-permute-done.5.refs_8_.refs_10_), channel_id=1, source_target_pairs={{0,8},{1,9},{2,10},{3,11},{4,12},{5,13},{6,14},{7,15},{8,0},{9,1},... | collective-permute-start | bytes 196616 | tf_op jit(solution)/shard_map/ppermute | solution.py:28
  22.3 4.0 %collective-permute-start.10 = (f32[16,512]{1,0:T(8,128)S(1)}, f32[16,512]{1,0:T(8,128)S(1)}, u32[]{:S(2)}, u32[]{:S(2)}) collective-permute-start(f32[16,512]{1,0:T(8,128)S(1)} %get-tuple-element.24.refs_0_.refs_3_), channel_id=1, source_target_pairs={{0,16},{1,17},{2,18},{3,19},{4,20},{5,21},{6,22},{7,23},{8,24},{9,... | collective-permute-start | bytes 98312 | tf_op jit(solution)/shard_map/ppermute | solution.py:28
  23.8 3.9 %collective-permute-start.11 = (f32[16,512]{1,0:T(8,128)S(1)}, f32[16,512]{1,0:T(8,128)S(1)}, u32[]{:S(2)}, u32[]{:S(2)}) collective-permute-start(f32[16,512]{1,0:T(8,128)S(1)} %get-tuple-element.24.refs_0_.refs_3_), channel_id=1, source_target_pairs={{0,1},{1,0},{2,3},{3,2},{4,5},{5,4},{6,7},{7,6},{8,9},{9,8},{10,11... | collective-permute-start | bytes 98312 | tf_op jit(solution)/shard_map/ppermute | solution.py:28
  25.3 4.8 %collective-permute-start.12 = (f32[16,512]{1,0:T(8,128)S(1)}, f32[16,512]{1,0:T(8,128)S(1)}, u32[]{:S(2)}, u32[]{:S(2)}) collective-permute-start(f32[16,512]{1,0:T(8,128)S(1)} %get-tuple-element.24.refs_0_.refs_3_), channel_id=1, source_target_pairs={{0,17},{1,16},{2,19},{3,18},{4,21},{5,20},{6,23},{7,22},{8,25},{9,... | collective-permute-start | bytes 98312 | tf_op jit(solution)/shard_map/ppermute | solution.py:28
  34.4 15.5 %collective-permute-start.19 = (bf16[512,256]{1,0:T(8,128)(2,1)S(1)}, bf16[512,256]{1,0:T(8,128)(2,1)S(1)}, u32[]{:S(2)}, u32[]{:S(2)}) collective-permute-start(bf16[512,256]{1,0:T(8,128)(2,1)S(1)} %get-tuple-element.37), channel_id=1, source_target_pairs={{0,8},{1,9},{2,10},{3,11},{4,12},{5,13},{6,14},{7,15},{8,0},{9,1},... | collective-permute-start | bytes 786440 | tf_op jit(solution)/shard_map/ppermute | solution.py:28
  34.5 6.4 %collective-permute-start.13 = (bf16[128,512]{1,0:T(8,128)(2,1)S(1)}, bf16[128,512]{1,0:T(8,128)(2,1)S(1)}, u32[]{:S(2)}, u32[]{:S(2)}) collective-permute-start(bf16[128,512]{1,0:T(8,128)(2,1)S(1)} %get-tuple-element.26), channel_id=1, source_target_pairs={{0,16},{1,17},{2,18},{3,19},{4,20},{5,21},{6,22},{7,23},{8,24},{9,... | collective-permute-start | bytes 393224 | tf_op jit(solution)/shard_map/ppermute | solution.py:28
  35.1 11.3 %collective-permute-start.14 = (bf16[128,512]{1,0:T(8,128)(2,1)S(1)}, bf16[128,512]{1,0:T(8,128)(2,1)S(1)}, u32[]{:S(2)}, u32[]{:S(2)}) collective-permute-start(bf16[128,512]{1,0:T(8,128)(2,1)S(1)} %get-tuple-element.27), channel_id=1, source_target_pairs={{0,1},{1,0},{2,3},{3,2},{4,5},{5,4},{6,7},{7,6},{8,9},{9,8},{10,11... | collective-permute-start | bytes 393224 | tf_op jit(solution)/shard_map/ppermute | solution.py:28
  35.6 13.0 %collective-permute-start.15 = (bf16[128,512]{1,0:T(8,128)(2,1)S(1)}, bf16[128,512]{1,0:T(8,128)(2,1)S(1)}, u32[]{:S(2)}, u32[]{:S(2)}) collective-permute-start(bf16[128,512]{1,0:T(8,128)(2,1)S(1)} %get-tuple-element.28), channel_id=1, source_target_pairs={{0,17},{1,16},{2,19},{3,18},{4,21},{5,20},{6,23},{7,22},{8,25},{9,... | collective-permute-start | bytes 393224 | tf_op jit(solution)/shard_map/ppermute | solution.py:28
  38.0 12.9 %collective-permute-start.18 = (bf16[128,512]{1,0:T(8,128)(2,1)S(1)}, bf16[128,512]{1,0:T(8,128)(2,1)S(1)}, u32[]{:S(2)}, u32[]{:S(2)}) collective-permute-start(bf16[128,512]{1,0:T(8,128)(2,1)S(1)} %get-tuple-element.35), channel_id=1, source_target_pairs={{0,17},{1,16},{2,19},{3,18},{4,21},{5,20},{6,23},{7,22},{8,25},{9,... | collective-permute-start | bytes 393224 | tf_op jit(solution)/shard_map/ppermute | solution.py:28
  40.9 13.5 %collective-permute-start.17 = (bf16[128,512]{1,0:T(8,128)(2,1)S(1)}, bf16[128,512]{1,0:T(8,128)(2,1)S(1)}, u32[]{:S(2)}, u32[]{:S(2)}) collective-permute-start(bf16[128,512]{1,0:T(8,128)(2,1)S(1)} %get-tuple-element.34), channel_id=1, source_target_pairs={{0,1},{1,0},{2,3},{3,2},{4,5},{5,4},{6,7},{7,6},{8,9},{9,8},{10,11... | collective-permute-start | bytes 393224 | tf_op jit(solution)/shard_map/ppermute | solution.py:28
  46.4 8.1 %collective-permute-start.16 = (bf16[128,512]{1,0:T(8,128)(2,1)S(1)}, bf16[128,512]{1,0:T(8,128)(2,1)S(1)}, u32[]{:S(2)}, u32[]{:S(2)}) collective-permute-start(bf16[128,512]{1,0:T(8,128)(2,1)S(1)} %get-tuple-element.33), channel_id=1, source_target_pairs={{0,16},{1,17},{2,18},{3,19},{4,20},{5,21},{6,22},{7,23},{8,24},{9,... | collective-permute-start | bytes 393224 | tf_op jit(solution)/shard_map/ppermute | solution.py:28
  50.0 6.3 %collective-permute-start.22 = (bf16[128,256]{1,0:T(8,128)(2,1)S(1)}, bf16[128,256]{1,0:T(8,128)(2,1)S(1)}, u32[]{:S(2)}, u32[]{:S(2)}) collective-permute-start(bf16[128,256]{1,0:T(8,128)(2,1)S(1)} %get-tuple-element.41), channel_id=1, source_target_pairs={{0,6},{1,7},{2,4},{3,5},{4,2},{5,3},{6,0},{7,1},{8,14},{9,15},{10,... | collective-permute-start | bytes 196616 | tf_op jit(solution)/shard_map/ppermute | solution.py:28
  50.8 6.6 %collective-permute-start.21 = (bf16[128,256]{1,0:T(8,128)(2,1)S(1)}, bf16[128,256]{1,0:T(8,128)(2,1)S(1)}, u32[]{:S(2)}, u32[]{:S(2)}) collective-permute-start(bf16[128,256]{1,0:T(8,128)(2,1)S(1)} %get-tuple-element.42), channel_id=1, source_target_pairs={{0,4},{1,5},{2,6},{3,7},{4,0},{5,1},{6,2},{7,3},{8,12},{9,13},{10,... | collective-permute-start | bytes 196616 | tf_op jit(solution)/shard_map/ppermute | solution.py:28
  51.0 6.4 %collective-permute-start.20 = (bf16[128,256]{1,0:T(8,128)(2,1)S(1)}, bf16[128,256]{1,0:T(8,128)(2,1)S(1)}, u32[]{:S(2)}, u32[]{:S(2)}) collective-permute-start(bf16[128,256]{1,0:T(8,128)(2,1)S(1)} %get-tuple-element.40), channel_id=1, source_target_pairs={{0,2},{1,3},{2,0},{3,1},{4,6},{5,7},{6,4},{7,5},{8,10},{9,11},{10,... | collective-permute-start | bytes 196616 | tf_op jit(solution)/shard_map/ppermute | solution.py:28
